TPU v7x, 32 devices: a whole 2x2x4 slice. The times are simulated.
32 devices in a mesh: shard: 4 (over x, core), ctx: 2 (over y), tp: 4 (over z).
Axes of the slice: x: 2, y: 2, z: 4, core: 2. Of those that a mesh axis runs over, the one named last changes fastest.
Arguments:
- tokens: bfloat16 [1024, 16, 1024], P(('ctx', 'tp'), 'shard'), may hold values from -6 to 6
- segments: int32 [16, 1024], P('shard'), may hold values from 0 to 1, never falling along the last dimension, each value on 1 to 800 neighbouring positions
- encoder: bfloat16 [384, 16, 1024], P(None, 'shard'), may hold values from -6 to 6
- norm_self: float32 [1024], replicated, may hold values from 0.5 to 1.5
- norm_cross: float32 [1024], replicated, may hold values from 0.5 to 1.5
- norm_ffn: float32 [1024], replicated, may hold values from 0.5 to 1.5
- rel_table: float32 [32, 16], P(None, 'tp'), may hold values from -4 to 4
- self_query: bfloat16 [1024, 1024], P(('shard', 'ctx'), 'tp'), may hold values from -0.09375 to 0.09375
- self_key: bfloat16 [1024, 1024], P(('shard', 'ctx'), 'tp'), may hold values from -0.09375 to 0.09375
- self_value: bfloat16 [1024, 1024], P(('shard', 'ctx'), 'tp'), may hold values from -0.1875 to 0.1875
- self_out: bfloat16 [1024, 1024], P('tp', ('shard', 'ctx')), may hold values from -1 to 1
- cross_query: bfloat16 [1024, 1024], P(('shard', 'ctx'), 'tp'), may hold values from -0.09375 to 0.09375
- cross_key: bfloat16 [1024, 1024], P(('shard', 'ctx'), 'tp'), may hold values from -0.09375 to 0.09375
- cross_value: bfloat16 [1024, 1024], P(('shard', 'ctx'), 'tp'), may hold values from -0.1875 to 0.1875
- cross_out: bfloat16 [1024, 1024], P('tp', ('shard', 'ctx')), may hold values from -1 to 1
- ffn_gate: bfloat16 [1024, 2816], P(('shard', 'ctx'), 'tp'), may hold values from -0.1875 to 0.1875
- ffn_up: bfloat16 [1024, 2816], P(('shard', 'ctx'), 'tp'), may hold values from -0.1875 to 0.1875
- ffn_down: bfloat16 [2816, 1024], P('tp', ('shard', 'ctx')), may hold values from -0.109375 to 0.109375
- cotangent: bfloat16 [1024, 16, 1024], P(('ctx', 'tp'), 'shard'), may hold values from -6 to 6
Outputs:
- result: bfloat16 [1024, 16, 1024], P(('ctx', 'tp'), 'shard')
- tokens_grad: float32 [1024, 16, 1024], P(('ctx', 'tp'), 'shard')
- encoder_grad: float32 [384, 16, 1024], P('ctx', 'shard', 'tp')
- norm_self_grad: float32 [1024], replicated
- norm_cross_grad: float32 [1024], replicated
- norm_ffn_grad: float32 [1024], replicated
- rel_table_grad: float32 [32, 16], P(('shard', 'ctx'), 'tp')
- self_query_grad: float32 [1024, 1024], P(('shard', 'ctx'), 'tp')
- self_key_grad: float32 [1024, 1024], P(('shard', 'ctx'), 'tp')
- self_value_grad: float32 [1024, 1024], P(('shard', 'ctx'), 'tp')
- self_out_grad: float32 [1024, 1024], P('tp', ('shard', 'ctx'))
- cross_query_grad: float32 [1024, 1024], P(('shard', 'ctx'), 'tp')
- cross_key_grad: float32 [1024, 1024], P(('shard', 'ctx'), 'tp')
- cross_value_grad: float32 [1024, 1024], P(('shard', 'ctx'), 'tp')
- cross_out_grad: float32 [1024, 1024], P('tp', ('shard', 'ctx'))
- ffn_gate_grad: float32 [1024, 2816], P(('shard', 'ctx'), 'tp')
- ffn_up_grad: float32 [1024, 2816], P(('shard', 'ctx'), 'tp')
- feedforward_down_gradient: float32 [2816, 1024], P('tp', ('shard', 'ctx'))
Inputs may be any that keep to these rules, and one draw needn't show every extreme that they name: `segments`: within each sequence the document numbers never fall; every document holds 1 to 800 tokens.
All inputs are finite; a program needn't handle non-finite values.
Results may differ from a plain program's by a relative error of at most 0.028.
The roundings to bfloat16 on the way count: a program that leaves them out, or rounds other values in their place, can miss the bound.
Values may be sent and summed in bfloat16 or wider, within the bound.
No kernel may reach another device: no remote copies, remote signals or barrier semaphores. Data moves between devices by JAX's collectives and lax.ppermute only.
A program may use at most 320 MiB of HBM per device.

v0:
```python
from functools import partial, reduce

import jax
import jax.numpy as jnp
from jax import lax
from jax.experimental import pallas as pl
from jax.experimental.pallas import tpu as pltpu
from jax.sharding import PartitionSpec as P

MICRO = 4
SHARD, CTX, TP = AXES = ("shard", "ctx", "tp")

BF = jnp.bfloat16
F32 = jnp.float32


def nt(a, b):
    return lax.dot_general(a, b, (((1,), (1,)), ((), ())), preferred_element_type=F32)


def nn(a, b):
    return lax.dot_general(a, b, (((1,), (0,)), ((), ())), preferred_element_type=F32)


def tn(a, b):
    return lax.dot_general(a, b, (((0,), (0,)), ((), ())), preferred_element_type=F32)


def toeplitz(line, half):
    wide = jnp.broadcast_to(line, (half, 2 * half))
    return pltpu.roll(wide, 0, 1, stride=1, stride_axis=0)[:, :half]


def diagonals(tile, half):
    blank = jnp.zeros((8, half), F32)
    total = jnp.zeros((8, 2 * half), F32)
    for at in range(0, half, 8):
        wide = jnp.concatenate([tile[at : at + 8, :], blank], axis=1)
        total = total + (pltpu.roll(wide, 2 * half - at, 1) if at else wide)
    return total


def lane_pick(first, second, left):
    return jnp.where(left, first, second)


def row_softmax(tiles):
    peak = jnp.max(tiles[0], axis=1, keepdims=True)
    for tile in tiles[1:]:
        peak = jnp.maximum(peak, jnp.max(tile, axis=1, keepdims=True))
    exps = [jnp.exp(tile - peak) for tile in tiles]
    total = jnp.sum(reduce_add(exps), axis=1, keepdims=True)
    scale = 1.0 / total
    return [(e * scale).astype(BF) for e in exps], peak + jnp.log(total)


def reduce_add(parts):
    out = parts[0]
    for part in parts[1:]:
        out = out + part
    return out


def self_forward_kernel(core, q, k_own, v_own, k_far, v_far, lines, mask, out, logs):
    half = q.shape[0] // 2
    left = lax.broadcasted_iota(jnp.int32, (1, q.shape[1]), 1) < q.shape[1] // 2
    swapped = core[0] == 1
    a, b = slice(0, half), slice(half, 2 * half)
    outs, totals = [], []
    for head in range(2):
        keep = left if head == 0 else jnp.logical_not(left)
        qh = jnp.where(keep, q[...], jnp.zeros((), BF))
        near = toeplitz(lines[0, 2 * head : 2 * head + 1, :], half)
        next_tile = toeplitz(lines[0, 2 * head + 1 : 2 * head + 2, :], half)
        far = lines[0, 4 + head : 5 + head, :half]
        qa, qb = qh[a], qh[b]
        ka, kb, xa, xb = k_own[a, :], k_own[b, :], k_far[a, :], k_far[b, :]
        pa, la = row_softmax(
            [
                nt(qa, ka) + near + mask[a, 0:half],
                nt(qa, xa) + next_tile + mask[a, 2 * half : 3 * half],
            ]
        )
        oa = nn(pa[0], v_own[a, :]) + nn(pa[1], v_far[a, :])
        pb, lb = row_softmax(
            [
                nt(qb, ka) + jnp.where(swapped, next_tile, far) + mask[b, 0:half],
                nt(qb, kb) + near + mask[b, half : 2 * half],
                nt(qb, xa) + far + mask[b, 2 * half : 3 * half],
                nt(qb, xb) + next_tile + mask[b, 3 * half : 4 * half],
            ]
        )
        ob = (
            nn(pb[0], v_own[a, :])
            + nn(pb[1], v_own[b, :])
            + nn(pb[2], v_far[a, :])
            + nn(pb[3], v_far[b, :])
        )
        outs.append((oa, ob))
        totals.append((la, lb))
    out[a, :] = lane_pick(outs[0][0], outs[1][0], left).astype(BF)
    out[b, :] = lane_pick(outs[0][1], outs[1][1], left).astype(BF)
    for at, piece in ((0, a), (1, b)):
        turned = lane_pick(totals[0][at], totals[1][at], left).T
        logs[0, 0:1, piece] = turned[0:1, :]
        logs[0, 1:2, piece] = turned[q.shape[1] // 2 : q.shape[1] // 2 + 1, :]


def self_backward_kernel(
    core, q, k_own, v_own, k_far, v_far, grad, lines, mask, logs,
    dq, own_out, far_out, sums,
):
    half = q.shape[0] // 2
    left = lax.broadcasted_iota(jnp.int32, (1, q.shape[1]), 1) < q.shape[1] // 2
    swapped = core[0] == 1
    a, b = slice(0, half), slice(half, 2 * half)
    keys = {"oa": (k_own, v_own, a, 0), "ob": (k_own, v_own, b, 1), "xa": (k_far, v_far, a, 2), "xb": (k_far, v_far, b, 3)}
    dk, dv, dqs = {}, {}, [None, None]
    for head in range(2):
        keep = left if head == 0 else jnp.logical_not(left)
        zero = jnp.zeros((), BF)
        qh = jnp.where(keep, q[...], zero)
        gh = jnp.where(keep, grad[...], zero)
        near = toeplitz(lines[0, 2 * head : 2 * head + 1, :], half)
        next_tile = toeplitz(lines[0, 2 * head + 1 : 2 * head + 2, :], half)
        far = lines[0, 4 + head : 5 + head, :half]
        held = {}
        for at, piece, plan in (
            (0, a, (("oa", near), ("xa", next_tile))),
            (1, b, (("oa", jnp.where(swapped, next_tile, far)), ("ob", near), ("xa", far), ("xb", next_tile))),
        ):
            qp, gp = qh[piece], gh[piece]
            total = logs[0, head : head + 1, piece]
            probs, dots = [], []
            for name, bias in plan:
                k, v, rows, slot = keys[name]
                score = nt(k[rows, :], qp) + bias + mask[slot * half : (slot + 1) * half, piece]
                probs.append(jnp.exp(score - total))
                dots.append(nt(v[rows, :], gp))
            delta = jnp.sum(reduce_add([p * d for p, d in zip(probs, dots)]), axis=0, keepdims=True)
            for (name, _), p, d in zip(plan, probs, dots):
                k, v, rows, slot = keys[name]
                ds = p * (d - delta)
                held[at, name] = ds
                low = ds.astype(BF)
                dvp, dkp = nn(p.astype(BF), gp), nn(low, qp)
                dv[name] = dvp if name not in dv else dv[name] + dvp
                dk[name] = dkp if name not in dk else dk[name] + dkp
                dqp = tn(low, jnp.where(keep, k[rows, :], zero))
                dqs[at] = dqp if dqs[at] is None else dqs[at] + dqp
        base = 32 * head
        sums[0, base : base + 8, :] = diagonals(held[0, "oa"] + held[1, "ob"], half)
        sums[0, base + 8 : base + 16, :] = diagonals(held[0, "xa"] + held[1, "xb"], half)
        sums[0, base + 16 : base + 24, :] = diagonals(held[1, "oa"], half)
        rest = reduce_add([held[1, "xa"][at : at + 8, :] for at in range(0, half, 8)])
        sums[0, base + 24 : base + 32, :] = jnp.concatenate([rest, jnp.zeros_like(rest)], axis=1)
    dq[a, :] = dqs[0].astype(BF)
    dq[b, :] = dqs[1].astype(BF)
    sub = pl.multiple_of(lax.rem(pl.program_id(0), 2) * 128, 128)
    for name, ref, rows in (("oa", own_out, a), ("ob", own_out, b), ("xa", far_out, a), ("xb", far_out, b)):
        ref[rows, pl.ds(sub, 128)] = dk[name].astype(BF)
        ref[rows, pl.ds(sub + 256, 128)] = dv[name].astype(BF)


def self_specs(rows):
    kv = lambda which: (lambda p, c: (0, (p // 2) * 4 + which * 2 + p % 2))
    q = pl.BlockSpec((rows, 128), lambda p, c: (0, p))
    k = pl.BlockSpec((rows, 128), kv(0))
    v = pl.BlockSpec((rows, 128), kv(1))
    small = pl.BlockSpec((1, 8, rows), lambda p, c: (p, 0, 0))
    return q, k, v, small


def self_forward(core, q, kv_own, kv_far, lines, mask):
    rows, width = q.shape
    pairs = width // 128
    qs, ks, vs, small = self_specs(rows)
    return pl.pallas_call(
        self_forward_kernel,
        grid_spec=pltpu.PrefetchScalarGridSpec(
            num_scalar_prefetch=1,
            grid=(pairs,),
            in_specs=[qs, ks, vs, ks, vs, small, pl.BlockSpec((rows, 2 * rows), lambda p, c: (0, 0))],
            out_specs=[qs, small],
        ),
        out_shape=(
            jax.ShapeDtypeStruct((rows, width), BF),
            jax.ShapeDtypeStruct((pairs, 8, rows), F32),
        ),
        cost_estimate=pl.CostEstimate(flops=pairs * 24 * 65536 * 128 * 2, bytes_accessed=10 << 20, transcendentals=0),
        name="self_fwd",
    )(core, q, kv_own, kv_own, kv_far, kv_far, lines, mask)


def self_backward(core, q, kv_own, kv_far, grad, lines, mask_t, logs):
    rows, width = q.shape
    pairs = width // 128
    qs, ks, vs, small = self_specs(rows)
    wide = pl.BlockSpec((rows, 512), lambda p, c: (0, p // 2))
    return pl.pallas_call(
        self_backward_kernel,
        grid_spec=pltpu.PrefetchScalarGridSpec(
            num_scalar_prefetch=1,
            grid=(pairs,),
            in_specs=[qs, ks, vs, ks, vs, qs, small, pl.BlockSpec((2 * rows, rows), lambda p, c: (0, 0)), small],
            out_specs=[qs, wide, wide, pl.BlockSpec((1, 64, rows), lambda p, c: (p, 0, 0))],
        ),
        out_shape=(
            jax.ShapeDtypeStruct((rows, width), BF),
            jax.ShapeDtypeStruct((rows, 2 * width), BF),
            jax.ShapeDtypeStruct((rows, 2 * width), BF),
            jax.ShapeDtypeStruct((pairs, 64, rows), F32),
        ),
        cost_estimate=pl.CostEstimate(flops=pairs * 60 * 65536 * 128 * 2, bytes_accessed=20 << 20, transcendentals=0),
        name="self_bwd",
    )(core, q, kv_own, kv_own, kv_far, kv_far, grad, lines, mask_t, logs)


def cross_forward_kernel(q, k, v, out, logs):
    left = lax.broadcasted_iota(jnp.int32, (1, q.shape[1]), 1) < q.shape[1] // 2
    outs, totals = [], []
    for head in range(2):
        keep = left if head == 0 else jnp.logical_not(left)
        qh = jnp.where(keep, q[...], jnp.zeros((), BF))
        p, total = row_softmax([nt(qh, k[...])])
        outs.append(nn(p[0], v[...]))
        totals.append(total)
    out[...] = lane_pick(outs[0], outs[1], left).astype(BF)
    turned = lane_pick(totals[0], totals[1], left).T
    logs[0, 0:1, :] = turned[0:1, :]
    logs[0, 1:2, :] = turned[q.shape[1] // 2 : q.shape[1] // 2 + 1, :]


def cross_backward_kernel(q, k, v, grad, logs, dq, out):
    left = lax.broadcasted_iota(jnp.int32, (1, q.shape[1]), 1) < q.shape[1] // 2
    dqs = dks = dvs = None
    zero = jnp.zeros((), BF)
    for head in range(2):
        keep = left if head == 0 else jnp.logical_not(left)
        qh = jnp.where(keep, q[...], zero)
        gh = jnp.where(keep, grad[...], zero)
        p = jnp.exp(nt(k[...], qh) - logs[0, head : head + 1, :])
        d = nt(v[...], gh)
        delta = jnp.sum(p * d, axis=0, keepdims=True)
        low = (p * (d - delta)).astype(BF)
        dvp, dkp, dqp = nn(p.astype(BF), gh), nn(low, qh), tn(low, jnp.where(keep, k[...], zero))
        dqs = dqp if dqs is None else dqs + dqp
        dks = dkp if dks is None else dks + dkp
        dvs = dvp if dvs is None else dvs + dvp
    dq[...] = dqs.astype(BF)
    sub = pl.multiple_of(lax.rem(pl.program_id(0), 2) * 128, 128)
    out[:, pl.ds(sub, 128)] = dks.astype(BF)
    out[:, pl.ds(sub + 256, 128)] = dvs.astype(BF)


def cross_specs(rows, states):
    kv = lambda which: (lambda p: (0, (p // 2) * 4 + which * 2 + p % 2))
    q = pl.BlockSpec((rows, 128), lambda p: (0, p))
    k = pl.BlockSpec((states, 128), kv(0))
    v = pl.BlockSpec((states, 128), kv(1))
    small = pl.BlockSpec((1, 8, rows), lambda p: (p, 0, 0))
    return q, k, v, small


def cross_forward(q, kv):
    rows, width = q.shape
    states = kv.shape[0]
    pairs = width // 128
    qs, ks, vs, small = cross_specs(rows, states)
    return pl.pallas_call(
        cross_forward_kernel,
        grid=(pairs,),
        in_specs=[qs, ks, vs],
        out_specs=[qs, small],
        out_shape=(
            jax.ShapeDtypeStruct((rows, width), BF),
            jax.ShapeDtypeStruct((pairs, 8, rows), F32),
        ),
        cost_estimate=pl.CostEstimate(flops=pairs * 8 * rows * states * 128, bytes_accessed=4 << 20, transcendentals=0),
        name="cross_fwd",
    )(q, kv, kv)


def cross_backward(q, kv, grad, logs):
    rows, width = q.shape
    states = kv.shape[0]
    pairs = width // 128
    qs, ks, vs, small = cross_specs(rows, states)
    return pl.pallas_call(
        cross_backward_kernel,
        grid=(pairs,),
        in_specs=[qs, ks, vs, qs, small],
        out_specs=[qs, pl.BlockSpec((states, 512), lambda p: (0, p // 2))],
        out_shape=(
            jax.ShapeDtypeStruct((rows, width), BF),
            jax.ShapeDtypeStruct((states, 2 * width), BF),
        ),
        cost_estimate=pl.CostEstimate(flops=pairs * 20 * rows * states * 128, bytes_accessed=6 << 20, transcendentals=0),
        name="cross_bwd",
    )(q, kv, kv, grad, logs)


def staged_kernel(body, weights, n_blocks, n_tiled, n_whole, n_out, *refs):
    core_refs = refs[:n_blocks]
    at = n_blocks
    tiled, at = refs[at : at + n_tiled], at + n_tiled
    whole, at = refs[at : at + n_whole], at + n_whole
    outs, at = refs[at : at + n_out], at + n_out
    held, sems = refs[at : at + len(weights)], refs[at + len(weights) :]
    first = pl.program_id(0) == 0
    copies = []
    for (colors, start, size), store, sem in zip(weights, held, sems):
        own = []
        for color, blocks in enumerate(colors):
            for slot, block in enumerate(blocks):
                own.append(
                    pltpu.make_async_copy(
                        core_refs[block].at[:, start : start + size, :],
                        store.at[:, color * size : (color + 1) * size, slot * 128 : (slot + 1) * 128],
                        sem.at[color * 8 + slot],
                    )
                )
        copies.append(own)

    @pl.when(first)
    def _():
        for own in copies:
            for copy in own:
                copy.start()

    ready = set()

    def weight(which):
        if which not in ready:
            ready.add(which)

            @pl.when(first)
            def _():
                for copy in copies[which]:
                    copy.wait()

        value = held[which][...]
        return value.reshape(-1, value.shape[-1])

    body(first, weight, tiled, whole, outs)


def staged(body, weights, tiled, whole, out_types, tile, flops):
    flat, index = [], {}
    plan = []
    for colors, start, size in weights:
        for blocks in colors:
            for block in blocks:
                if id(block) not in index:
                    index[id(block)] = len(flat)
                    flat.append(block)
        plan.append(([[index[id(b)] for b in blocks] for blocks in colors], start, size))
    rows = tiled[0].shape[0]

    def tile_spec(shape):
        return pl.BlockSpec((tile, shape[1]), lambda m: (m, 0))

    def whole_spec(shape):
        return pl.BlockSpec(shape, lambda m: (0,) * len(shape))

    out_specs, out_shapes = [], []
    for shape, dtype in out_types:
        out_shapes.append(jax.ShapeDtypeStruct(shape, dtype))
        if len(shape) == 3:
            out_specs.append(pl.BlockSpec((shape[0], tile, shape[2]), lambda m: (0, m, 0)))
        else:
            out_specs.append(tile_spec(shape) if shape[0] == rows else whole_spec(shape))
    nbytes = sum(v.size * v.dtype.itemsize for v in (*flat, *tiled, *whole))
    return pl.pallas_call(
        partial(staged_kernel, body, plan, len(flat), len(tiled), len(whole), len(out_types)),
        grid=(rows // tile,),
        in_specs=[pl.BlockSpec(memory_space=pl.ANY)] * len(flat)
        + [tile_spec(v.shape) for v in tiled]
        + [whole_spec(v.shape) for v in whole],
        out_specs=out_specs,
        out_shape=out_shapes,
        scratch_shapes=[
            pltpu.VMEM((4, len(colors) * size, 1024), BF) for colors, start, size in plan
        ]
        + [pltpu.SemaphoreType.DMA((8 * len(colors),)) for colors, start, size in plan],
        cost_estimate=pl.CostEstimate(flops=flops, bytes_accessed=nbytes, transcendentals=0),
    )(*flat, *tiled, *whole)


def unit(h):
    return lax.rsqrt(jnp.mean(h * h, axis=-1, keepdims=True) + epsilon)


def normed(h, gain):
    return (h * unit(h) * gain).astype(BF)


def norm_pull(h, gain, grad):
    scale = unit(h)
    inner = gain * grad
    mean = jnp.mean(inner * h, axis=-1, keepdims=True)
    back = scale * inner - h * (scale * scale * scale) * mean
    return back, jnp.sum(grad * h * scale, axis=0, keepdims=True)


def add_up(first, out, value):
    @pl.when(first)
    def _():
        out[...] = value

    @pl.when(jnp.logical_not(first))
    def _():
        out[...] = out[...] + value


def kv_body(first, weight, tiled, whole, outs):
    n = normed(tiled[0][...].astype(F32), whole[0][...])
    outs[0][...] = n
    outs[1][...] = nt(n, weight(0)).astype(BF)


def nt_body(first, weight, tiled, whole, outs):
    outs[0][...] = nt(tiled[0][...], weight(0)).astype(BF)


def nn_body(first, weight, tiled, whole, outs):
    outs[0][...] = nn(tiled[0][...], weight(0)).astype(BF)


def mid_body(first, weight, tiled, whole, outs):
    mixed, resid = tiled
    after = resid[...].astype(F32) + nn(mixed[...], weight(0))
    outs[0][...] = after
    n = normed(after, whole[0][...])
    outs[1][...] = n
    if len(outs) > 2:
        outs[2][...] = nt(n, weight(1)).astype(BF)


GELU_SCALE = (2.0 / 3.141592653589793) ** 0.5


def feed_body(first, weight, tiled, whole, outs):
    n, g, before, grad_before = tiled
    sides_out, after_out, normed_out = outs
    gate = nt(n[...], weight(0))
    up = nt(n[...], weight(1))
    square = gate * gate
    wave = jnp.tanh(GELU_SCALE * gate * (1.0 + 0.044715 * square))
    soft = 0.5 * (1.0 + wave)
    act = gate * soft
    hidden = (act * up).astype(BF)
    sides_out[2] = hidden
    after_out[...] = (before[...].astype(F32) + nn(hidden, weight(2))).astype(after_out.dtype)
    grad = nt(g[...], weight(2))
    slope = soft + 0.5 * gate * (1.0 - wave * wave) * (GELU_SCALE * (1.0 + 3 * 0.044715 * square))
    grad_gate = (grad * up * slope).astype(BF)
    grad_up = (grad * act).astype(BF)
    sides_out[0] = grad_gate
    sides_out[1] = grad_up
    normed_out[...] = grad_before[...] + nn(grad_gate, weight(0)) + nn(grad_up, weight(1))


def turn_body(first, weight, tiled, whole, outs):
    h, grad_normed, grad_out = tiled
    back, gain_part = norm_pull(h[...], whole[0][...], grad_normed[...])
    total = grad_out[...].astype(F32) + back
    low = total.astype(BF)
    outs[0][...] = total
    outs[1][...] = low
    outs[2][...] = nt(low, weight(0)).astype(BF)
    add_up(first, outs[3], gain_part)


def second_turn_body(first, weight, tiled, whole, outs):
    grad_query, h, grad_out = tiled
    back, gain_part = norm_pull(h[...], whole[0][...], nn(grad_query[...], weight(0)))
    total = grad_out[...].astype(F32) + back
    low = total.astype(BF)
    outs[0][...] = total
    outs[1][...] = low
    outs[2][...] = nt(low, weight(1)).astype(BF)
    add_up(first, outs[3], gain_part)


def last_body(first, weight, tiled, whole, outs):
    grad_query, grad_kv, h, grad_out = tiled
    grad_normed = nn(grad_query[...], weight(0)) + nn(grad_kv[...], weight(1))
    back, gain_part = norm_pull(h[...].astype(F32), whole[0][...], grad_normed)
    outs[0][...] = (grad_out[...] + back).astype(BF)
    add_up(first, outs[1], gain_part)


def grads_kernel(size, ways, kept, two, *refs):
    n_colors = len(ways)
    last = pl.program_id(0) == pl.num_programs(0) - 1
    if two:
        rows_grad = jnp.where(last, refs[1][...], refs[0][...])
    else:
        rows_grad = refs[0][0]
    refs = refs[1 + two :]
    came = refs[2 : 2 + n_colors] if kept else ()
    outs = refs[2 + len(came) :]
    value = tn(rows_grad, jnp.where(last, refs[1][...], refs[0][...]))
    for color, bit in enumerate(ways):
        for z in range(4):
            row = (z * n_colors + color) * size
            piece = value[row : row + size]
            for at in range(4):
                part = piece[:, at * 128 : (at + 1) * 128]
                if not kept:
                    outs[color][at, z] = part.astype(BF)
                    continue
                part = (part + came[color][at, z].astype(F32)).astype(BF)
                if at & bit:
                    outs[2 * color][at // 3, z] = part
                else:
                    outs[2 * color + 1][min(at, 1), z] = part


def weight_grads(rows_grad, first_in, second_in, size, ways, came=None):
    two = isinstance(rows_grad, tuple)
    if two:
        (rows, inner), count = rows_grad[0].shape, 2
        sources = list(rows_grad)
        source_specs = [pl.BlockSpec((rows, inner), lambda w: (0, 0))] * 2
    else:
        count, rows, inner = rows_grad.shape
        sources = [rows_grad]
        source_specs = [pl.BlockSpec((1, rows, inner), lambda w: (w, 0, 0))]
    kept = came is not None
    slab = pl.BlockSpec((4, 4, size, 128), lambda w: (0, 0, w, 0))
    pair = pl.BlockSpec((2, 4, size, 128), lambda w: (0, 0, w, 0))
    side = pl.BlockSpec((rows, 512), lambda w: (0, 0 if kept else 1))
    if kept:
        out_specs = [pair] * (2 * len(ways))
        out_shape = [jax.ShapeDtypeStruct((2, 4, count * size, 128), BF)] * (2 * len(ways))
    else:
        out_specs = [slab] * len(ways)
        out_shape = [jax.ShapeDtypeStruct((4, 4, count * size, 128), BF)] * len(ways)
    extra = list(came) if kept else []
    return pl.pallas_call(
        partial(grads_kernel, size, ways, kept, two),
        grid=(count,),
        in_specs=source_specs + [side, side] + [slab] * len(extra),
        out_specs=out_specs,
        out_shape=out_shape,
        cost_estimate=pl.CostEstimate(
            flops=2 * count * rows * inner * 512,
            bytes_accessed=2 * count * inner * (rows + 1024),
            transcendentals=0,
        ),
    )(*sources, first_in, second_in, *extra)


def near_sum_kernel(*refs):
    count = len(refs) // 3
    for at in range(count):
        refs[2 * count + at][...] = refs[2 * at][0] + refs[2 * at + 1][0]


def near_sums(kept, came):
    shape = kept[0].shape
    second = pl.BlockSpec((1, *shape[1:]), lambda m: (1, 0, 0, 0))
    out = pl.BlockSpec(shape[1:], lambda m: (0, 0, 0))
    operands = [v for both in zip(kept, came) for v in both]
    return pl.pallas_call(
        near_sum_kernel,
        grid=(1,),
        in_specs=[second] * len(operands),
        out_specs=[out] * len(kept),
        out_shape=[jax.ShapeDtypeStruct(shape[1:], BF)] * len(kept),
        cost_estimate=pl.CostEstimate(flops=0, bytes_accessed=6 * kept[0].size, transcendentals=0),
        name="s1",
    )(*operands)


def far_sum_kernel(*refs):
    out = refs[-1]
    count = len(refs) // 3
    size = out.shape[1] // count
    for at in range(count):
        total = refs[3 * at][0].astype(F32) + refs[3 * at + 1][0].astype(F32)
        total = total + refs[3 * at + 2][...].astype(F32)
        out[:, at * size : (at + 1) * size, :] = total.astype(BF)


def far_sums(kept, came, last):
    shape = kept[0].shape
    first = pl.BlockSpec((1, *shape[1:]), lambda m: (0, 0, 0, 0))
    whole = pl.BlockSpec(shape[1:], lambda m: (0, 0, 0))
    operands = [v for both in zip(kept, came, last) for v in both]
    total = (shape[1], shape[2] * len(kept), shape[3])
    return pl.pallas_call(
        far_sum_kernel,
        grid=(1,),
        in_specs=[first, first, whole] * len(kept),
        out_specs=pl.BlockSpec(total, lambda m: (0, 0, 0)),
        out_shape=jax.ShapeDtypeStruct(total, BF),
        cost_estimate=pl.CostEstimate(flops=0, bytes_accessed=8 * kept[0].size, transcendentals=0),
        name="s2",
    )(*operands)


def gather_rows_kernel(place, *refs):
    got, out, sem = refs[:4], refs[4], refs[5]
    sx, core, y, z = place[0], place[1], place[2], place[3]
    copies = []
    for step in range(4):
        row = pl.multiple_of(lax.rem(z + 4 - step, 4) ^ (2 * core), 1) * 128
        for at in range(8):
            lane = 128 * ((((at >> 1) & 1) ^ sx) * 4 + ((at >> 2) ^ core) * 2 + ((at & 1) ^ y))
            copies.append(
                pltpu.make_async_copy(
                    got[step].at[:, pl.ds(pl.multiple_of(lane, 128), 128)],
                    out.at[pl.ds(pl.multiple_of(row, 128), 128), at * 128 : (at + 1) * 128],
                    sem.at[step * 8 + at],
                )
            )
    for copy in copies:
        copy.start()
    for copy in copies:
        copy.wait()


def gather_rows_call(place, got):
    rows, width = got[0].shape
    return pl.pallas_call(
        gather_rows_kernel,
        grid_spec=pltpu.PrefetchScalarGridSpec(
            num_scalar_prefetch=1,
            grid=(1,),
            in_specs=[pl.BlockSpec(memory_space=pl.ANY)] * 4,
            out_specs=pl.BlockSpec((4 * rows, width), lambda m, p: (0, 0)),
            scratch_shapes=[pltpu.SemaphoreType.DMA((32,))],
        ),
        out_shape=jax.ShapeDtypeStruct((4 * rows, width), got[0].dtype),
        cost_estimate=pl.CostEstimate(flops=0, bytes_accessed=16 * rows * width, transcendentals=0),
        name="rows_in",
    )(place, *got)


def scatter_rows_kernel(place, rows_ref, *refs):
    outs, sem = refs[:4], refs[4]
    sx, core, y, z = place[0], place[1], place[2], place[3]
    copies = []
    for step in range(4):
        row = (lax.rem(z + 4 - step, 4) ^ (2 * core)) * 128
        for at in range(8):
            lane = 128 * ((((at >> 1) & 1) ^ sx) * 4 + ((at >> 2) ^ core) * 2 + ((at & 1) ^ y))
            copies.append(
                pltpu.make_async_copy(
                    rows_ref.at[pl.ds(pl.multiple_of(row, 128), 128), at * 128 : (at + 1) * 128],
                    outs[step].at[:, pl.ds(pl.multiple_of(lane, 128), 128)],
                    sem.at[step * 8 + at],
                )
            )
    for copy in copies:
        copy.start()
    for copy in copies:
        copy.wait()


def scatter_rows_call(place, rows_in):
    rows, width = rows_in.shape
    part = jax.ShapeDtypeStruct((rows // 4, width), rows_in.dtype)
    return pl.pallas_call(
        scatter_rows_kernel,
        grid_spec=pltpu.PrefetchScalarGridSpec(
            num_scalar_prefetch=1,
            grid=(1,),
            in_specs=[pl.BlockSpec(memory_space=pl.ANY)],
            out_specs=[pl.BlockSpec((rows // 4, width), lambda m, p: (0, 0))] * 4,
            scratch_shapes=[pltpu.SemaphoreType.DMA((32,))],
        ),
        out_shape=[part] * 4,
        cost_estimate=pl.CostEstimate(flops=0, bytes_accessed=4 * rows * width, transcendentals=0),
        name="rows_out",
    )(place, rows_in)


epsilon = 1e-06
masked_score = -1000000000.0
bucket_edges = (19, 21, 24, 27, 31, 35, 40, 46, 52, 59, 67, 77, 87, 99, 113)


def from_behind(x, axis, by):
    peers = lax.axis_size(axis)
    pairs = [(i, i + by) for i in range(peers) if 0 <= i + by < peers]
    return lax.ppermute(x, axis, pairs)


def bucket_index(distance):
    distance = jnp.maximum(distance, 0)
    far_bucket = reduce(
        lambda running, threshold: running + (distance >= threshold).astype(jnp.int32),
        bucket_edges,
        jnp.full(distance.shape, 16, jnp.int32),
    )
    return jnp.where(distance < 16, distance, far_bucket)


def rms_scale(hidden_in):
    return lax.rsqrt(jnp.mean(hidden_in * hidden_in, axis=-1, keepdims=True) + epsilon)


def norm_back(hidden_in, gain_vec, grad_in):
    inv_scale = rms_scale(hidden_in)
    scaled_grad = gain_vec * grad_in
    inner_mean = jnp.mean(scaled_grad * hidden_in, axis=-1, keepdims=True)
    grad_back = (
        inv_scale * scaled_grad - hidden_in * (inv_scale * inv_scale * inv_scale) * inner_mean
    )
    gain_part = jnp.sum(grad_in * hidden_in * inv_scale, axis=(0, 1))
    return (grad_back, gain_part)


def soft_rows(scores):
    peak = jnp.max(scores, axis=-1, keepdims=True)
    exp_scores = jnp.exp(scores - peak)
    row_total = jnp.sum(exp_scores, axis=-1, keepdims=True)
    return (exp_scores / row_total, peak + jnp.log(row_total))


def soft_back(attn_probs, grad_probs):
    return attn_probs * (grad_probs - jnp.sum(attn_probs * grad_probs, axis=-1, keepdims=True))


def spread_bias(bias_line, row_count, col_count):
    row_width = row_count + col_count
    head_total = bias_line.shape[0]
    tiled_line = jnp.tile(bias_line, (1, row_count))[:, : row_count * row_width]
    return tiled_line.reshape(head_total, row_count, row_width)[:, :, :col_count]


def fold_bias(score_grid, row_count, col_count):
    row_width = row_count + col_count
    head_total = score_grid.shape[0]
    padded = jnp.pad(score_grid, ((0, 0), (0, 0), (0, row_count))).reshape(
        head_total, row_count * row_width
    )
    padded = jnp.pad(padded, ((0, 0), (0, row_count))).reshape(head_total, row_count, row_width + 1)
    return jnp.sum(padded, axis=1)


def gather_rows(normed):
    return lax.all_gather(normed, TP, axis=0, tiled=True)


def gather_grads(grad_in):
    return lax.all_gather(grad_in, TP, axis=0, tiled=True)


def branch_sum(input_values, input_weight):
    return lax.psum_scatter(
        jnp.einsum("gci,iu->gcu", input_values, input_weight, preferred_element_type=jnp.float32),
        TP,
        scatter_dimension=0,
        tiled=True,
    )


def input_sum(incoming_gradients, input_weight):
    return lax.psum_scatter(
        jnp.einsum(
            "iyv,mv->iym", incoming_gradients, input_weight, preferred_element_type=jnp.float32
        ),
        TP,
        scatter_dimension=0,
        tiled=True,
    )


def cross_scores(queries_in, states_kv, head_count):
    local_len, seq_count, head_width = queries_in.shape
    state_len = states_kv.shape[0]
    queries_h = queries_in.reshape(local_len, seq_count, head_count, -1)
    keys_h = states_kv[..., :head_width].reshape(state_len, seq_count, head_count, -1)
    values_h = states_kv[..., head_width:].reshape(state_len, seq_count, head_count, -1)
    scores = jnp.einsum("qshe,kshe->shqk", queries_h, keys_h, preferred_element_type=jnp.float32)
    return (scores, queries_h, keys_h, values_h)


def micro_step(
    tokens, segments, encoder, cotangent, norm_self, norm_cross, norm_ffn, rel_table, shards
):
    gathered = (
        lax.all_gather(shards[0], (SHARD, CTX), axis=0, tiled=True),
        lax.all_gather(shards[1], (SHARD, CTX), axis=0, tiled=True),
        lax.all_gather(shards[2], (SHARD, CTX), axis=0, tiled=True),
        lax.all_gather(shards[3], (SHARD, CTX), axis=1, tiled=True),
        lax.all_gather(shards[4], (SHARD, CTX), axis=0, tiled=True),
        lax.all_gather(shards[5], (SHARD, CTX), axis=0, tiled=True),
        lax.all_gather(shards[6], (SHARD, CTX), axis=0, tiled=True),
        lax.all_gather(shards[7], (SHARD, CTX), axis=1, tiled=True),
        lax.all_gather(shards[8], (SHARD, CTX), axis=0, tiled=True),
        lax.all_gather(shards[9], (SHARD, CTX), axis=0, tiled=True),
        lax.all_gather(shards[10], (SHARD, CTX), axis=1, tiled=True),
    )
    (
        w_query,
        w_key,
        w_value,
        output_weight,
        cross_query_weight,
        c_key,
        c_value,
        cross_output_weight,
        w_gate,
        w_up,
        down_weight,
    ) = gathered
    own_rows = tokens.shape[0]
    seq_count = tokens.shape[1]
    local_len = own_rows * lax.axis_size(TP)
    window_len = 3 * local_len
    period = window_len + local_len + 1
    head_count = rel_table.shape[1]
    head_width = w_query.shape[1]
    feed_width = w_gate.shape[1]
    ctx_index = lax.axis_index(CTX)
    fill_ids = jnp.full((seq_count, 2 * local_len), -1, jnp.int32)
    seg_padded = jnp.concatenate([fill_ids, segments], axis=1)
    seg_window = lax.dynamic_slice_in_dim(seg_padded, ctx_index * local_len, window_len, 1)
    seg_query = lax.dynamic_slice_in_dim(segments, ctx_index * local_len, local_len, 1)
    offsets = jnp.arange(period, dtype=jnp.int32)
    distance = jnp.where(
        offsets < window_len, 2 * local_len - offsets, 2 * local_len - offsets + period
    )
    one_hot = (
        bucket_index(distance)[:, None] == jnp.arange(rel_table.shape[0], dtype=jnp.int32)[None, :]
    ).astype(jnp.float32)
    bias_line = jnp.dot(
        one_hot, rel_table, precision=lax.Precision.HIGHEST, preferred_element_type=jnp.float32
    ).T
    rel_bias = spread_bias(bias_line, local_len, window_len)
    causal_ok = (
        jnp.arange(window_len, dtype=jnp.int32)[None, :]
        <= jnp.arange(local_len, dtype=jnp.int32)[:, None] + 2 * local_len
    )

    def self_scores(one_query, one_window, query_ids, window_ids):
        queries_h = one_query.reshape(local_len, head_count, -1)
        keys_h = one_window[:, :head_width].reshape(window_len, head_count, -1)
        values_h = one_window[:, head_width:].reshape(window_len, head_count, -1)
        scores = (
            jnp.einsum("qhe,khe->hqk", queries_h, keys_h, preferred_element_type=jnp.float32)
            + rel_bias
        )
        allowed = (query_ids[:, None] == window_ids[None, :]) & causal_ok
        return (jnp.where(allowed[None], scores, masked_score), queries_h, keys_h, values_h)

    def self_forward(items):
        one_query, one_window, query_ids, window_ids = items
        scores, _, _, values_h = self_scores(one_query, one_window, query_ids, window_ids)
        attn_probs, log_total = soft_rows(scores)
        block_out = jnp.einsum(
            "hqk,khe->qhe",
            attn_probs.astype(jnp.bfloat16),
            values_h,
            preferred_element_type=jnp.float32,
        )
        return (block_out.reshape(local_len, head_width), log_total)

    def self_backward(items):
        one_query, one_window, query_ids, window_ids, log_total, grad_out = items
        scores, queries_h, keys_h, values_h = self_scores(
            one_query, one_window, query_ids, window_ids
        )
        attn_probs = jnp.exp(scores - log_total)
        grad_heads = grad_out.reshape(local_len, head_count, -1)
        grad_values = jnp.einsum(
            "hqk,qhe->khe",
            attn_probs.astype(jnp.bfloat16),
            grad_heads,
            preferred_element_type=jnp.float32,
        )
        grad_probs = jnp.einsum(
            "qhe,khe->hqk", grad_heads, values_h, preferred_element_type=jnp.float32
        )
        grad_scores = soft_back(attn_probs, grad_probs)
        grad_line = fold_bias(grad_scores, local_len, window_len)
        grad_low = grad_scores.astype(jnp.bfloat16)
        grad_queries = jnp.einsum(
            "hqk,khe->qhe", grad_low, keys_h, preferred_element_type=jnp.float32
        )
        grad_keys = jnp.einsum(
            "hqk,qhe->khe", grad_low, queries_h, preferred_element_type=jnp.float32
        )
        grad_pair = jnp.concatenate(
            [
                grad_keys.reshape(window_len, head_width),
                grad_values.reshape(window_len, head_width),
            ],
            axis=-1,
        )
        return (grad_queries.reshape(local_len, head_width), grad_pair, grad_line)

    resid_in = tokens.astype(jnp.float32)
    normed_one = (resid_in * rms_scale(resid_in) * norm_self).astype(jnp.bfloat16)
    first_rows = gather_rows(normed_one)
    self_attention_weight = jnp.concatenate([w_query, w_key, w_value], axis=1)
    projected = jnp.einsum(
        "rmh,ha->rma", first_rows, self_attention_weight, preferred_element_type=jnp.float32
    ).astype(jnp.bfloat16)
    queries = projected[..., :head_width]
    key_value = projected[..., head_width:]
    earlier = [from_behind(key_value, CTX, offset) for offset in (2, 1)]
    window = jnp.concatenate(earlier + [key_value], axis=0)
    seq_queries = jnp.moveaxis(queries, 1, 0)
    seq_window = jnp.moveaxis(window, 1, 0)
    self_mixed, self_logs = lax.map(self_forward, (seq_queries, seq_window, seg_query, seg_window))
    attended_rows = jnp.moveaxis(self_mixed, 0, 1).astype(jnp.bfloat16)
    after_self = resid_in + branch_sum(attended_rows, output_weight)
    normed_two = (after_self * rms_scale(after_self) * norm_cross).astype(jnp.bfloat16)
    second_rows = gather_rows(normed_two)
    cross_q = jnp.einsum(
        "rmh,ha->rma", second_rows, cross_query_weight, preferred_element_type=jnp.float32
    ).astype(jnp.bfloat16)
    state_weight = jnp.concatenate([c_key, c_value], axis=1)
    cross_kv = jnp.einsum(
        "rsd,df->rsf", encoder, state_weight, preferred_element_type=jnp.float32
    ).astype(jnp.bfloat16)
    scores, queries_h, keys_h, values_h = cross_scores(cross_q, cross_kv, head_count)
    attn_probs, cross_logs = soft_rows(scores)
    cross_mix = jnp.einsum(
        "shqk,kshe->qshe",
        attn_probs.astype(jnp.bfloat16),
        values_h,
        preferred_element_type=jnp.float32,
    )
    cross_attended = cross_mix.reshape(local_len, seq_count, head_width).astype(jnp.bfloat16)
    after_cross = after_self + branch_sum(cross_attended, cross_output_weight)
    normed_three = (after_cross * rms_scale(after_cross) * norm_ffn).astype(jnp.bfloat16)
    third_rows = gather_rows(normed_three)
    feedforward_weight = jnp.concatenate([w_gate, w_up], axis=1)
    gate_up_product = jnp.einsum(
        "rmh,ha->rma", third_rows, feedforward_weight, preferred_element_type=jnp.float32
    )
    gate_pre = gate_up_product[..., :feed_width]
    up_pre = gate_up_product[..., feed_width:]
    hidden_rows = (jax.nn.gelu(gate_pre, approximate=True) * up_pre).astype(jnp.bfloat16)
    result = after_cross + branch_sum(hidden_rows, down_weight)
    grad_result = cotangent.astype(jnp.float32)
    feedforward_gradient = gather_grads(grad_result.astype(jnp.bfloat16))
    feedforward_down_gradient = jnp.einsum(
        "euy,euh->yh", hidden_rows, feedforward_gradient, preferred_element_type=jnp.float32
    )
    hidden_gradient = jnp.einsum(
        "ezk,ck->ezc", feedforward_gradient, down_weight, preferred_element_type=jnp.float32
    )
    _, feed_pull = jax.vjp(
        lambda gate_in, up_in: jax.nn.gelu(gate_in, approximate=True) * up_in, gate_pre, up_pre
    )
    grad_gate, grad_up = feed_pull(hidden_gradient)
    gate_up_gradient = jnp.concatenate([grad_gate, grad_up], axis=-1).astype(jnp.bfloat16)
    feed_grads = jnp.einsum(
        "zvn,zvp->np", third_rows, gate_up_gradient, preferred_element_type=jnp.float32
    )
    ffn_gate_grad = feed_grads[:, :feed_width]
    ffn_up_grad = feed_grads[:, feed_width:]
    ffn_sums = None
    grad_back_three, gain_three = norm_back(
        after_cross, norm_ffn, input_sum(gate_up_gradient, feedforward_weight)
    )
    grad_mid = grad_result + grad_back_three
    cross_gradient = gather_grads(grad_mid.astype(jnp.bfloat16))
    cross_out_grad = jnp.einsum(
        "euy,euh->yh", cross_attended, cross_gradient, preferred_element_type=jnp.float32
    )
    grad_crossed = jnp.einsum(
        "ezk,ck->ezc", cross_gradient, cross_output_weight, preferred_element_type=jnp.float32
    ).astype(jnp.bfloat16)
    grad_heads = grad_crossed.reshape(local_len, seq_count, head_count, -1)
    cross_probs = jnp.exp(scores - cross_logs)
    grad_cvalues = jnp.einsum(
        "shqk,qshe->kshe",
        cross_probs.astype(jnp.bfloat16),
        grad_heads,
        preferred_element_type=jnp.float32,
    )
    grad_probs = jnp.einsum(
        "qshe,kshe->shqk", grad_heads, values_h, preferred_element_type=jnp.float32
    )
    grad_low = soft_back(cross_probs, grad_probs).astype(jnp.bfloat16)
    cross_query_weight_gradient = jnp.einsum(
        "shqk,kshe->qshe", grad_low, keys_h, preferred_element_type=jnp.float32
    )
    cross_query_weight_gradient = cross_query_weight_gradient.reshape(
        local_len, seq_count, head_width
    ).astype(jnp.bfloat16)
    grad_ckeys = jnp.einsum(
        "shqk,qshe->kshe", grad_low, queries_h, preferred_element_type=jnp.float32
    )
    state_len = encoder.shape[0]
    grad_ckv = jnp.concatenate(
        [
            grad_ckeys.reshape(state_len, seq_count, head_width),
            grad_cvalues.reshape(state_len, seq_count, head_width),
        ],
        axis=-1,
    )
    grad_ckv_own = lax.psum_scatter(
        grad_ckv.astype(jnp.bfloat16), CTX, scatter_dimension=0, tiled=True
    )
    state_rows = grad_ckv_own.shape[0]
    states_own = lax.dynamic_slice_in_dim(encoder, ctx_index * state_rows, state_rows, 0)
    state_grads = jnp.einsum(
        "rsd,rsf->df", states_own, grad_ckv_own, preferred_element_type=jnp.float32
    )
    cross_key_grad = state_grads[:, :head_width]
    cross_value_grad = state_grads[:, head_width:]
    state_term = jnp.einsum(
        "rsf,df->rsd", grad_ckv_own, state_weight, preferred_element_type=jnp.float32
    )
    encoder_grad = lax.psum_scatter(
        state_term.astype(jnp.bfloat16), TP, scatter_dimension=2, tiled=True
    ).astype(jnp.float32)
    cross_query_grad = jnp.einsum(
        "zvn,zvp->np", second_rows, cross_query_weight_gradient, preferred_element_type=jnp.float32
    )
    grad_back_two, gain_two = norm_back(
        after_self, norm_cross, input_sum(cross_query_weight_gradient, cross_query_weight)
    )
    grad_first = grad_mid + grad_back_two
    self_attention_gradient = gather_grads(grad_first.astype(jnp.bfloat16))
    self_out_grad = jnp.einsum(
        "euy,euh->yh", attended_rows, self_attention_gradient, preferred_element_type=jnp.float32
    )
    grad_attended = jnp.einsum(
        "ezk,ck->ezc", self_attention_gradient, output_weight, preferred_element_type=jnp.float32
    ).astype(jnp.bfloat16)
    grad_q, grad_window, grad_lines = lax.map(
        self_backward,
        (
            seq_queries,
            seq_window,
            seg_query,
            seg_window,
            self_logs,
            jnp.moveaxis(grad_attended, 1, 0),
        ),
    )
    table_grad = jnp.einsum(
        "tb,ht->bh",
        one_hot,
        jnp.sum(grad_lines, axis=0),
        precision=lax.Precision.HIGHEST,
        preferred_element_type=jnp.float32,
    )
    grad_window = jnp.moveaxis(grad_window, 0, 1)
    grad_kv = grad_window[2 * local_len :]
    for offset, grad_part in (
        (-2, grad_window[:local_len]),
        (-1, grad_window[local_len : 2 * local_len]),
    ):
        grad_kv = grad_kv + from_behind(grad_part.astype(jnp.bfloat16), CTX, offset).astype(
            grad_part.dtype
        )
    projection_gradient = jnp.concatenate([jnp.moveaxis(grad_q, 0, 1), grad_kv], axis=-1).astype(
        jnp.bfloat16
    )
    self_attention_gradients = jnp.einsum(
        "zvn,zvp->np", first_rows, projection_gradient, preferred_element_type=jnp.float32
    )
    self_query_grad = self_attention_gradients[:, :head_width]
    self_key_grad = self_attention_gradients[:, head_width : 2 * head_width]
    self_value_grad = self_attention_gradients[:, 2 * head_width :]
    grad_back_one, gain_one = norm_back(
        resid_in, norm_self, input_sum(projection_gradient, self_attention_weight)
    )
    tokens_grad = grad_first + grad_back_one
    local_grads = (
        self_query_grad,
        self_key_grad,
        self_value_grad,
        self_out_grad,
        cross_query_grad,
        cross_key_grad,
        cross_value_grad,
        cross_out_grad,
        ffn_gate_grad,
        ffn_up_grad,
        feedforward_down_gradient,
        table_grad,
    )
    return (
        result.astype(jnp.bfloat16),
        tokens_grad,
        encoder_grad,
        (gain_one, gain_two, gain_three),
        local_grads,
        ffn_sums,
    )


def body(
    tokens,
    segments,
    encoder,
    norm_self,
    norm_cross,
    norm_ffn,
    rel_table,
    self_query,
    self_key,
    self_value,
    self_out,
    cross_query,
    cross_key,
    cross_value,
    cross_out,
    ffn_gate,
    ffn_up,
    ffn_down,
    cotangent,
):
    shards = (
        self_query,
        self_key,
        self_value,
        self_out,
        cross_query,
        cross_key,
        cross_value,
        cross_out,
        ffn_gate,
        ffn_up,
        ffn_down,
    )
    per_micro = tokens.shape[1] // MICRO
    results = []
    token_grads = []
    state_grads = []
    gains = None
    totals = None
    for micro in range(MICRO):
        first = micro * per_micro
        out = micro_step(
            tokens[:, first : first + per_micro],
            segments[first : first + per_micro],
            encoder[:, first : first + per_micro],
            cotangent[:, first : first + per_micro],
            norm_self,
            norm_cross,
            norm_ffn,
            rel_table,
            shards,
        )
        results.append(out[0])
        token_grads.append(out[1])
        state_grads.append(out[2])
        gains = out[3] if gains is None else tuple((a + b for a, b in zip(gains, out[3])))
        totals = out[4] if totals is None else tuple((a + b for a, b in zip(totals, out[4])))
    gain_sums = lax.psum(gains, (SHARD, CTX, TP))
    summed = (
        lax.psum_scatter(
            totals[0].astype(jnp.bfloat16), (SHARD, CTX), scatter_dimension=0, tiled=True
        ).astype(jnp.float32),
        lax.psum_scatter(
            totals[1].astype(jnp.bfloat16), (SHARD, CTX), scatter_dimension=0, tiled=True
        ).astype(jnp.float32),
        lax.psum_scatter(
            totals[2].astype(jnp.bfloat16), (SHARD, CTX), scatter_dimension=0, tiled=True
        ).astype(jnp.float32),
        lax.psum_scatter(
            totals[3].astype(jnp.bfloat16), (SHARD, CTX), scatter_dimension=1, tiled=True
        ).astype(jnp.float32),
        lax.psum_scatter(
            totals[4].astype(jnp.bfloat16), (SHARD, CTX), scatter_dimension=0, tiled=True
        ).astype(jnp.float32),
        lax.psum_scatter(
            totals[5].astype(jnp.bfloat16), (SHARD, CTX), scatter_dimension=0, tiled=True
        ).astype(jnp.float32),
        lax.psum_scatter(
            totals[6].astype(jnp.bfloat16), (SHARD, CTX), scatter_dimension=0, tiled=True
        ).astype(jnp.float32),
        lax.psum_scatter(
            totals[7].astype(jnp.bfloat16), (SHARD, CTX), scatter_dimension=1, tiled=True
        ).astype(jnp.float32),
        lax.psum_scatter(
            totals[8].astype(jnp.bfloat16), (SHARD, CTX), scatter_dimension=0, tiled=True
        ).astype(jnp.float32),
        lax.psum_scatter(
            totals[9].astype(jnp.bfloat16), (SHARD, CTX), scatter_dimension=0, tiled=True
        ).astype(jnp.float32),
        lax.psum_scatter(
            totals[10].astype(jnp.bfloat16), (SHARD, CTX), scatter_dimension=1, tiled=True
        ).astype(jnp.float32),
        lax.psum_scatter(
            totals[11].astype(jnp.bfloat16), (SHARD, CTX), scatter_dimension=0, tiled=True
        ).astype(jnp.float32),
    )
    result = jnp.concatenate(results, axis=1)
    tokens_grad = jnp.concatenate(token_grads, axis=1)
    encoder_grad = jnp.concatenate(state_grads, axis=1)
    return (
        result,
        tokens_grad,
        encoder_grad,
        gain_sums[0],
        gain_sums[1],
        gain_sums[2],
        summed[11],
        summed[0],
        summed[1],
        summed[2],
        summed[3],
        summed[4],
        summed[5],
        summed[6],
        summed[7],
        summed[8],
        summed[9],
        summed[10],
    )


def chip_coords(index):
    return (index >> 4, (index >> 3) & 1, (index >> 2) & 1, index & 3)


def move(x, target):
    pairs = []
    for index in range(32):
        sx, core, y, z = target(*chip_coords(index))
        pairs.append((index, sx * 16 + core * 8 + y * 4 + z))
    return lax.ppermute(x, AXES, pairs)


def flip_x(v):
    return move(v, lambda sx, core, y, z: (1 - sx, core, y, z))


def flip_core(v):
    return move(v, lambda sx, core, y, z: (sx, 1 - core, y, z))


def flip_y(v):
    return move(v, lambda sx, core, y, z: (sx, core, 1 - y, z))


def from_z(v, step):
    return move(v, lambda sx, core, y, z: (sx, core, y, (z - step) % 4))


def my_coords():
    shard = lax.axis_index(SHARD)
    return (shard // 2, shard % 2, lax.axis_index(CTX), lax.axis_index(TP))


def swap_blocks(blocks, place):
    sx, core, y, _ = place
    for bit, mask in ((y, 1), (core, 2), (sx, 4)):
        taken = bit == 1
        blocks = [jnp.where(taken, blocks[at ^ mask], blocks[at]) for at in range(8)]
    return blocks


RELATIVE = (0, 1, 4, 5, 2, 3, 6, 7)


def lanes(v):
    width = v.shape[-1] // 8
    return [v[..., at * width : (at + 1) * width] for at in range(8)]


def to_relative(v, place):
    blocks = swap_blocks(lanes(v), place)
    return jnp.concatenate([blocks[at] for at in RELATIVE], axis=-1)


def from_relative(v, place):
    given = lanes(v)
    blocks = [given[RELATIVE.index(at)] for at in range(8)]
    return jnp.concatenate(swap_blocks(blocks, place), axis=-1)


def pick(stack, at):
    return lax.dynamic_index_in_dim(stack, at, 0, keepdims=False)


def send_rows(block, place):
    _, _, _, z = place
    by_seq = jnp.transpose(block, (1, 0, 2))
    return [
        move(
            pick(by_seq, (z + step) % 4),
            lambda sx, core, y, z, step=step: (sx, (z >> 1) ^ y, core, (z + step) % 4),
        )
        for step in range(4)
    ]


def send_back(slots):
    return [
        move(
            slots[step],
            lambda sx, core, y, z, step=step: (
                sx,
                y,
                core ^ (((z - step) % 4) >> 1),
                (z - step) % 4,
            ),
        )
        for step in range(4)
    ]


def place_back(got, place):
    z = place[3]
    stack = jnp.stack(got)
    return jnp.stack([pick(stack, (at - z) % 4) for at in range(4)], axis=1)


def settle(*values):
    return lax.optimization_barrier(values)


WAYS = ((flip_y, flip_x), (flip_x, flip_y))
BITS = (1, 2)


def spread(pieces):
    both = lax.all_gather(jnp.stack(pieces), TP, axis=1)
    return [both[0], both[1]]


def ordered(way, held, near, far, cores):
    if way[0] is flip_y:
        return [held, near, far[0], far[1]] + cores
    return [held, far[0], near, far[1], cores[0], cores[2], cores[1], cores[3]]


def collect(both):
    rows = both.shape[1] // 2
    both = lax.psum_scatter(both, TP, scatter_dimension=0)
    return [both[:rows], both[rows:]]


def fast_layer(
    tokens, segments, encoder, norm_self, norm_cross, norm_ffn, rel_table,
    self_query, self_key, self_value, self_out,
    cross_query, cross_key, cross_value, cross_out,
    ffn_gate, ffn_up, ffn_down, cotangent,
):
    place = my_coords()
    _, core, y, z = place
    spot = jnp.stack(place).astype(jnp.int32)
    core_id = spot[1:2]
    heads = rel_table.shape[1]
    inner = self_query.shape[1]
    feed = ffn_gate.shape[1]
    cut = feed // 4
    rows = tokens.shape[0] * 4
    half = rows // 2
    width = tokens.shape[2]

    def near_of(held):
        return [way[0](h) for way, h in zip(WAYS, held)]

    def far_of(held, near):
        return [[way[1](h), way[1](n)] for way, h, n in zip(WAYS, held, near)]

    def cores_of(values):
        return [flip_core(v) for v in values]

    def far_cores(far):
        return [cores_of(f) for f in far]

    def arrange(held, near, far, core_0, core_1, core_23):
        return [
            ordered(way, h, n, f, [a, b] + c)
            for way, h, n, f, a, b, c in zip(WAYS, held, near, far, core_0, core_1, core_23)
        ]

    pieces_s = [
        jnp.concatenate([self_key.T, self_value.T], axis=0),
        jnp.concatenate([self_query.T, self_out], axis=0),
    ]
    pieces_c = [
        jnp.concatenate([cross_key.T, cross_value.T], axis=0),
        jnp.concatenate([cross_query.T, cross_out], axis=0),
    ]
    gate_t, up_t = ffn_gate.T, ffn_up.T
    pieces_f = [
        [
            jnp.concatenate([w[at : at + cut] for w in (gate_t, up_t, ffn_down)], axis=0)
            for at in (2 * chunk * cut, (2 * chunk + 1) * cut)
        ]
        for chunk in (0, 1)
    ]
    mine = lax.dynamic_index_in_dim(encoder, z, 1, keepdims=False)
    mine_seg = lax.dynamic_index_in_dim(segments, z, 0, keepdims=True)
    pairs = []
    for index in range(32):
        ax, ac, ay, az = chip_coords(index)
        if ac == ay:
            pairs.append((index, ax * 16 + (1 - ac) * 8 + ay * 4 + az))

    held_s = spread(pieces_s)
    held_c = spread(pieces_c)
    held_f1 = spread(pieces_f[0])
    held_f2 = spread(pieces_f[1])
    held_s, rows_out, mine, mine_seg, rel_table = settle(held_s, tokens, mine, mine_seg, rel_table)
    near_s, core_s0 = near_of(held_s), cores_of(held_s)
    came_rows = send_rows(rows_out, place)
    came_enc = lax.ppermute(mine, AXES, pairs)
    came_seg = lax.ppermute(mine_seg, AXES, pairs)
    came_table = [from_z(rel_table, step) for step in (1, 2, 3)]
    near_s, core_s0 = settle(near_s, core_s0)
    far_s, core_s1 = far_of(held_s, near_s), cores_of(near_s)
    far_s, core_s1, held_c = settle(far_s, core_s1, held_c)
    core_s2 = far_cores(far_s)
    near_c, core_c0 = near_of(held_c), cores_of(held_c)
    near_c, core_c0, held_f1 = settle(near_c, core_c0, held_f1)
    far_c, core_c1 = far_of(held_c, near_c), cores_of(near_c)
    near_f1, core_f10 = near_of(held_f1), cores_of(held_f1)
    far_c, core_c1, near_f1, core_f10, held_f2, low_cotangent = settle(
        far_c, core_c1, near_f1, core_f10, held_f2, cotangent
    )
    core_c2 = far_cores(far_c)
    far_f1, core_f11 = far_of(held_f1, near_f1), cores_of(near_f1)
    near_f2, core_f20 = near_of(held_f2), cores_of(held_f2)
    came_grad = send_rows(low_cotangent, place)
    far_f1, core_f11, near_f2, core_f20, came_grad = settle(
        far_f1, core_f11, near_f2, core_f20, came_grad
    )
    core_f12 = far_cores(far_f1)
    far_f2, core_f21 = far_of(held_f2, near_f2), cores_of(near_f2)
    far_f2, core_f21 = settle(far_f2, core_f21)
    core_f22 = far_cores(far_f2)

    s_kv, s_qo = arrange(held_s, near_s, far_s, core_s0, core_s1, core_s2)
    c_kv, c_qo = arrange(held_c, near_c, far_c, core_c0, core_c1, core_c2)
    f_one = arrange(held_f1, near_f1, far_f1, core_f10, core_f11, core_f12)
    f_two = arrange(held_f2, near_f2, far_f2, core_f20, core_f21, core_f22)
    w_kv, w_ckv = ([s_kv], 0, 2 * inner), ([c_kv], 0, 2 * inner)
    w_q, w_so = ([s_qo], 0, inner), ([s_qo], inner, inner)
    w_cq, w_co = ([c_qo], 0, inner), ([c_qo], inner, inner)
    w_feed = [[(blocks, at * cut, cut) for at in range(3)] for blocks in (f_one, f_two)]

    resid = gather_rows_call(spot, came_rows)
    own_seq = core == y
    states = to_relative(jnp.where(own_seq, mine, came_enc), place)
    seg = jnp.where(own_seq, mine_seg, came_seg)[0]
    tables = jnp.stack([rel_table] + came_table)
    table = jnp.concatenate([pick(tables, (at - z) % 4) for at in range(4)], axis=1)
    gains = to_relative(jnp.stack([norm_self, norm_cross, norm_ffn]), place)
    gain_self, gain_cross, gain_ffn = gains[0:1], gains[1:2], gains[2:3]

    turn = jnp.arange(2 * half, dtype=jnp.int32)
    signed = jnp.where(turn < half, turn, turn - 2 * half)
    buckets = jnp.arange(table.shape[0], dtype=jnp.int32)

    def hot(distance):
        return (bucket_index(distance)[..., None] == buckets).astype(F32)

    def bias_lines(distance):
        return jnp.dot(
            hot(distance), table, precision=lax.Precision.HIGHEST, preferred_element_type=F32
        ).T

    def kernel_lines(sign):
        near = bias_lines(sign * signed).reshape(-1, 2, 2 * half)
        after = bias_lines(half + sign * signed).reshape(-1, 2, 2 * half)
        far = jnp.broadcast_to(table[-1].reshape(-1, 2, 1), near.shape)
        blank = jnp.zeros((near.shape[0], 2, 2 * half), F32)
        return jnp.concatenate(
            [near[:, 0:1], after[:, 0:1], near[:, 1:2], after[:, 1:2], far, blank], axis=1
        )

    lines_forward, lines_backward = kernel_lines(-1), kernel_lines(1)

    quarter = jnp.arange(half, dtype=jnp.int32)
    spots = jnp.concatenate([quarter + half * n for n in (core, 3 - core, 1 - core, 2 + core)])
    seg_spots = jnp.concatenate(
        [
            lax.dynamic_slice_in_dim(seg, half * n, half, 0)
            for n in (core, 3 - core, 1 - core, 2 + core)
        ]
    )

    def mask_of(query_at, key_at, query_seg, key_seg):
        return jnp.where((query_seg == key_seg) & (key_at <= query_at), 0.0, masked_score).astype(F32)

    mask = mask_of(spots[:rows, None], spots[None, :], seg_spots[:rows, None], seg_spots[None, :])
    mask_t = mask_of(spots[None, :rows], spots[:, None], seg_spots[None, :rows], seg_spots[:, None])

    tall = min(256, rows)
    dot = 2 * rows * width

    def full(count, dtype=BF):
        return ((rows, count), dtype)

    gain_out = ((1, width), F32)

    normed_self, kv_own = staged(
        kv_body, [w_kv], [resid], [gain_self],
        [full(width), full(2 * width)], tall, dot * 2 * width,
    )
    kv_far = flip_core(kv_own)
    (queries,) = staged(nt_body, [w_q], [normed_self], [], [full(width)], tall, dot * width)
    mixed, self_logs = self_forward(core_id, queries, kv_own, kv_far, lines_forward, mask)
    (cross_kv,) = staged(
        nt_body, [w_ckv], [states], [],
        [((states.shape[0], 2 * width), BF)], states.shape[0], dot * width,
    )
    after_self, normed_cross, cross_q = staged(
        mid_body, [w_so, w_cq], [mixed, resid], [gain_cross],
        [full(width, F32), full(width), full(width)], tall, dot * 2 * width,
    )
    cross_mixed, cross_logs = cross_forward(cross_q, cross_kv)
    after_cross, normed_ffn = staged(
        mid_body, [w_co], [cross_mixed, after_self], [gain_ffn],
        [full(width, F32), full(width)], tall, dot * width,
    )
    grad_low = gather_rows_call(spot, came_grad)
    total, grad_normed = after_cross, jnp.zeros((rows, width), F32)
    feed_sides, feed_over = [], []
    for chunk in (0, 1):
        sides, total, grad_normed = staged(
            feed_body, w_feed[chunk], [normed_ffn, grad_low, total, grad_normed], [],
            [((3, rows, 8 * cut), BF), full(width, BF if chunk else F32), full(width, F32)],
            tall, dot * 6 * 8 * cut,
        )
        away = weight_grads(sides, normed_ffn, grad_low, cut, BITS)
        feed_sides.append(sides)
        feed_over.append(cores_of(away))
    result_slots = scatter_rows_call(spot, total)

    def feed_jobs(chunk):
        return weight_grads(feed_sides[chunk], normed_ffn, grad_low, cut, BITS, feed_over[chunk])

    def first_stage(jobs):
        return [way[0](sent) for way, sent in zip(WAYS, jobs[0::2])]

    def second_stage(jobs, came):
        return [way[1](h) for way, h in zip(WAYS, near_sums(jobs[1::2], came))]

    def finish(jobs, came, last):
        return collect(far_sums(jobs[1::2], came, last))

    grad_mid, low_mid, grad_cross_mixed, gain_three = staged(
        turn_body, [w_co], [after_cross, grad_normed, grad_low], [gain_ffn],
        [full(width, F32), full(width), full(width), gain_out], tall, dot * width,
    )
    grad_cq, shared = cross_backward(cross_q, cross_kv, grad_cross_mixed, cross_logs)
    own_states = states.shape[0] // 2
    sent = lax.dynamic_slice_in_dim(shared, (1 - core) * own_states, own_states, 0)
    kept = lax.dynamic_slice_in_dim(shared, core * own_states, own_states, 0)
    grad_ckv = kept + flip_core(sent)
    states_own = lax.dynamic_slice_in_dim(states, core * own_states, own_states, 0)
    grad_first, low_first, grad_mixed, gain_two = staged(
        second_turn_body, [w_cq, w_so], [grad_cq, after_self, grad_mid], [gain_cross],
        [full(width, F32), full(width), full(width), gain_out], tall, dot * 2 * width,
    )
    pair_c = (grad_cq, cross_mixed)
    away_c = weight_grads(grad_ckv[None], states_own, states_own, 2 * inner, BITS[:1])
    away_c += weight_grads(pair_c, normed_cross, low_mid, inner, BITS[1:])
    over_c = cores_of(away_c)
    (state_grad,) = staged(
        nn_body, [w_ckv], [grad_ckv], [],
        [((own_states, width), BF)], own_states, dot * width,
    )
    grad_q, kv_kept, kv_sent, sums = self_backward(
        core_id, queries, kv_own, kv_far, grad_mixed, lines_backward, mask_t, self_logs
    )
    grad_kv = kv_kept + flip_core(kv_sent)
    pair_s = (grad_q, mixed)
    away_s = weight_grads(pair_s, normed_self, low_first, inner, BITS[1:])
    away_s = weight_grads(grad_kv[None], normed_self, normed_self, 2 * inner, BITS[:1]) + away_s
    over_s = cores_of(away_s)
    tokens_rows, gain_one = staged(
        last_body, [w_q, w_kv], [grad_q, grad_kv, resid, grad_first], [gain_self],
        [full(width), gain_out], tall, dot * 3 * width,
    )
    token_slots = scatter_rows_call(spot, tokens_rows)

    def cross_jobs():
        first = weight_grads(
            grad_ckv[None], states_own, states_own, 2 * inner, BITS[:1], over_c[:1]
        )
        return first + weight_grads(pair_c, normed_cross, low_mid, inner, BITS[1:], over_c[1:])

    def self_jobs():
        first = weight_grads(
            grad_kv[None], normed_self, normed_self, 2 * inner, BITS[:1], over_s[:1]
        )
        return first + weight_grads(pair_s, normed_self, low_first, inner, BITS[1:], over_s[1:])

    jobs_f1 = feed_jobs(0)
    n1 = first_stage(jobs_f1)
    n1, jobs_f2 = settle(n1, feed_jobs(1))
    n2 = second_stage(jobs_f1, n1)
    done_f1 = finish(jobs_f1, n1, n2)
    n1 = first_stage(jobs_f2)
    n1, result_slots, jobs_c = settle(n1, result_slots, cross_jobs())
    n2 = second_stage(jobs_f2, n1)
    back_result = send_back(result_slots)
    done_f2 = finish(jobs_f2, n1, n2)
    n1 = first_stage(jobs_c)
    n1, done_f1 = settle(n1, done_f1)
    jobs_s = self_jobs()
    n2 = second_stage(jobs_c, n1)
    done_c = finish(jobs_c, n1, n2)
    state_abs = from_relative(state_grad, place)
    state_cols = jnp.stack([state_abs[:, at * inner : (at + 1) * inner] for at in range(4)])
    got = [
        move(
            pick(state_cols, (z + step) % 4),
            lambda sx, core, y, z, step=step: (sx, y, core, (z + step) % 4),
        )
        for step in range(4)
    ]
    n1 = first_stage(jobs_s)
    n1, done_f2 = settle(n1, done_f2)
    back_tokens = send_back(token_slots)
    n2 = second_stage(jobs_s, n1)
    n2, done_c = settle(n2, done_c)
    sum_s = far_sums(jobs_s[1::2], n1, n2)

    inside = (signed[None, :] - jnp.arange(8, dtype=jnp.int32)[:, None]) % (2 * half)
    inside = jnp.where(inside < half, inside, inside - 2 * half)
    kinds = jnp.stack(
        [inside, half + inside, (3 - 2 * core) * half + inside, jnp.full_like(inside, 2 * half)]
    )
    sums = sums.reshape(4 * heads, 4, 8, 2 * half)
    table_grad = jnp.einsum(
        "ndmb,hndm->bh",
        hot(kinds),
        sums,
        precision=lax.Precision.HIGHEST,
        preferred_element_type=F32,
    )
    by_z = table_grad.reshape(-1, 4, heads)
    gain_parts = from_relative(jnp.concatenate([gain_one, gain_two, gain_three]), place)
    small = jnp.concatenate([gain_parts.reshape(-1), by_z.reshape(-1)]).reshape(-1, 128)
    sum_s, small = settle(sum_s, small)
    done_s = collect(sum_s)
    for flip in (
        flip_core,
        flip_x,
        flip_y,
        lambda v: move(v, lambda sx, core, y, z: (sx, core, y, z ^ 1)),
        lambda v: move(v, lambda sx, core, y, z: (sx, core, y, z ^ 2)),
    ):
        small = small + flip(small)
    small = small.reshape(-1)
    gain_sums = small[: gain_parts.size].reshape(gain_parts.shape)
    table_sum = small[gain_parts.size :].reshape(by_z.shape)
    block = lax.axis_index(SHARD) * 2 + y
    own_table = lax.dynamic_slice_in_dim(
        lax.dynamic_index_in_dim(table_sum, z, 1, keepdims=False), block * 4, 4, 0
    )
    result = place_back(back_result, place)
    tokens_grad = place_back(back_tokens, place).astype(F32)
    got = jnp.stack(got)
    encoder_grad = jnp.stack([pick(got, (z - at) % 4) for at in range(4)], axis=1).astype(F32)
    done_f1, done_f2, done_c, done_s = (
        [v.astype(F32) for v in done] for done in (done_f1, done_f2, done_c, done_s)
    )
    feed_done = [*done_f1, *done_f2]
    gate_grad, up_grad, down_grad = (
        jnp.concatenate([done[at * cut : (at + 1) * cut] for done in feed_done], axis=0)
        for at in range(3)
    )
    (kv_done, qo_done), (ckv_done, cqo_done) = done_s, done_c
    return (
        result,
        tokens_grad,
        encoder_grad,
        gain_sums[0],
        gain_sums[1],
        gain_sums[2],
        own_table,
        qo_done[:inner].T,
        kv_done[:inner].T,
        kv_done[inner:].T,
        qo_done[inner:],
        cqo_done[:inner].T,
        ckv_done[:inner].T,
        ckv_done[inner:].T,
        cqo_done[inner:],
        gate_grad.T,
        up_grad.T,
        down_grad,
    )


def fast_body(*args):
    return fast_layer(*args)


def solution(mesh):
    placed = (
        P((CTX, TP), SHARD, None),
        P(SHARD, None),
        P(None, SHARD, None),
        P(),
        P(),
        P(),
        P(None, TP),
        P((SHARD, CTX), TP),
        P((SHARD, CTX), TP),
        P((SHARD, CTX), TP),
        P(TP, (SHARD, CTX)),
        P((SHARD, CTX), TP),
        P((SHARD, CTX), TP),
        P((SHARD, CTX), TP),
        P(TP, (SHARD, CTX)),
        P((SHARD, CTX), TP),
        P((SHARD, CTX), TP),
        P(TP, (SHARD, CTX)),
        P((CTX, TP), SHARD, None),
    )
    fits = tuple(mesh.shape[axis] for axis in AXES) == (4, 2, 4)
    return jax.shard_map(
        fast_body if fits else body,
        mesh=mesh,
        in_specs=placed,
        out_specs=(
            P((CTX, TP), SHARD, None),
            P((CTX, TP), SHARD, None),
            P(CTX, SHARD, TP),
            P(),
            P(),
            P(),
            P((SHARD, CTX), TP),
            P((SHARD, CTX), TP),
            P((SHARD, CTX), TP),
            P((SHARD, CTX), TP),
            P(TP, (SHARD, CTX)),
            P((SHARD, CTX), TP),
            P((SHARD, CTX), TP),
            P((SHARD, CTX), TP),
            P(TP, (SHARD, CTX)),
            P((SHARD, CTX), TP),
            P((SHARD, CTX), TP),
            P(TP, (SHARD, CTX)),
        ),
        check_vma=False,
    )
```

profile of v0, /device:TPU:0, one launch (start us, length us, event | category | flops | bytes accessed | tf_op | source)
XLA Modules:
  0.0 730.5 jit_solution(7620276099575695183)
XLA Ops:
  23.8 19.0 %all-gather.9.cloned.1.call-done = bf16[2,2048,128]{2,1,0:T(8,128)(2,1)} async-done(((bf16[2,512,128]{2,1,0:T(8,128)(2,1)}), bf16[2,2048,128]{2,1,0:T(8,128)(2,1)}) %all-gather.9.cloned.1.call-update) | async-done | bytes 1048592 | tf_op jit(solution)/shard_map/all_gather | solution.py:1325
  47.9 10.7 %collective-permute-done.1.refs_1_.refs_9_ = bf16[4,512,128]{2,1,0:T(8,128)(2,1)} collective-permute-done((bf16[4,512,128]{2,1,0:T(8,128)(2,1)S(1)}, bf16[4,512,128]{2,1,0:T(8,128)(2,1)}, u32[]{:S(2)}, u32[]{:S(2)}) %collective-permute-start.1) | collective-permute-done | bytes 524320 | tf_op jit(solution)/shard_map/ppermute | solution.py:1228
  60.1 8.5 %collective-permute-done.2.refs_2_.refs_10_ = bf16[4,512,128]{2,1,0:T(8,128)(2,1)S(1)} collective-permute-done((bf16[4,512,128]{2,1,0:T(8,128)(2,1)S(1)}, bf16[4,512,128]{2,1,0:T(8,128)(2,1)S(1)}, u32[]{:S(2)}, u32[]{:S(2)}) %collective-permute-start.2) | collective-permute-done | bytes 524320 | tf_op jit(solution)/shard_map/ppermute | solution.py:1228
  117.0 20.6 %collective-permute-done.50.refs_2_ = bf16[128,1024]{1,0:T(8,128)(2,1)S(1)} collective-permute-done((bf16[128,1024]{1,0:T(8,128)(2,1)}, bf16[128,1024]{1,0:T(8,128)(2,1)S(1)}, u32[]{:S(2)}, u32[]{:S(2)}) %collective-permute-start.50) | collective-permute-done | bytes 262176 | tf_op jit(solution)/shard_map/ppermute | solution.py:1228
  141.3 11.9 %collective-permute-done.17.refs_11_.refs_3_ = bf16[4,512,128]{2,1,0:T(8,128)(2,1)S(1)} collective-permute-done((bf16[4,512,128]{2,1,0:T(8,128)(2,1)}, bf16[4,512,128]{2,1,0:T(8,128)(2,1)S(1)}, u32[]{:S(2)}, u32[]{:S(2)}) %collective-permute-start.17) | collective-permute-done | bytes 524320 | tf_op jit(solution)/shard_map/ppermute | solution.py:1228
  172.9 8.2 %collective-permute-start.35 = (bf16[128,1024]{1,0:T(8,128)(2,1)}, bf16[128,1024]{1,0:T(8,128)(2,1)S(1)}, u32[]{:S(2)}, u32[]{:S(2)}) collective-permute-start(bf16[128,1024]{1,0:T(8,128)(2,1)} %get-tuple-element.442), channel_id=1, source_target_pairs={{0,1},{1,2},{2,11},{3,8},{4,9},{5,10},{6,3},{7,0},{8,5},{9,6},{10,... | collective-permute-start | bytes 786440 | tf_op jit(solution)/shard_map/ppermute | solution.py:1228
  187.4 13.5 %collective-permute-start.36 = (bf16[128,1024]{1,0:T(8,128)(2,1)}, bf16[128,1024]{1,0:T(8,128)(2,1)S(1)}, u32[]{:S(2)}, u32[]{:S(2)}) collective-permute-start(bf16[128,1024]{1,0:T(8,128)(2,1)} %get-tuple-element.441), channel_id=1, source_target_pairs={{0,2},{1,3},{2,8},{3,9},{4,10},{5,11},{6,0},{7,1},{8,6},{9,7},{10,... | collective-permute-start | bytes 786440 | tf_op jit(solution)/shard_map/ppermute | solution.py:1228
  201.8 10.3 %collective-permute-done.36.refs_2_ = bf16[128,1024]{1,0:T(8,128)(2,1)S(1)} collective-permute-done((bf16[128,1024]{1,0:T(8,128)(2,1)}, bf16[128,1024]{1,0:T(8,128)(2,1)S(1)}, u32[]{:S(2)}, u32[]{:S(2)}) %collective-permute-start.36) | collective-permute-done | bytes 262176 | tf_op jit(solution)/shard_map/ppermute | solution.py:1228
  222.0 7.6 %shard_map.322 = (bf16[512,1024]{1,0:T(8,128)(2,1)}, bf16[512,2048]{1,0:T(8,128)(2,1)}) custom-call(bf16[4,512,128]{2,1,0:T(8,128)(2,1)} %bitcast.199, bf16[4,512,128]{2,1,0:T(8,128)(2,1)} %collective-permute-done.1.refs_1_.refs_9_, bf16[4,512,128]{2,1,0:T(8,128)(2,1)} %copy-done.39, bf16[4,512,128]{2,1,0:T(8,128)(2,1)} %collective-permute-done.5.refs_3_.refs_11_, ...), custom_call_target="tpu_custom_call" | custom-call | flops 2147483648 | bytes 5246976 | tf_op jit(solution)/shard_map/pallas_call | solution.py:374
  239.5 9.7 %collective-permute-done.64.refs_2_ = bf16[4,528,128]{2,1,0:T(8,128)(2,1)S(1)} collective-permute-done((bf16[4,528,128]{2,1,0:T(8,128)(2,1)S(1)}, bf16[4,528,128]{2,1,0:T(8,128)(2,1)S(1)}, u32[]{:S(2)}, u32[]{:S(2)}) %collective-permute-start.64) | collective-permute-done | bytes 540704 | tf_op jit(solution)/shard_map/ppermute | solution.py:1228
  250.8 9.3 %collective-permute-done.65.refs_3_ = bf16[4,528,128]{2,1,0:T(8,128)(2,1)} collective-permute-done((bf16[4,528,128]{2,1,0:T(8,128)(2,1)}, bf16[4,528,128]{2,1,0:T(8,128)(2,1)}, u32[]{:S(2)}, u32[]{:S(2)}) %collective-permute-start.65) | collective-permute-done | bytes 540704 | tf_op jit(solution)/shard_map/ppermute | solution.py:1228
  278.1 23.2 %self_fwd.1 = (bf16[512,1024]{1,0:T(8,128)(2,1)}, f32[8,8,512]{2,1,0:T(8,128)}) custom-call(s32[1]{0:T(128)} %bitcast.29.core, bf16[512,1024]{1,0:T(8,128)(2,1)} %shard_map.323.q, bf16[512,2048]{1,0:T(8,128)(2,1)} %get-tuple-element.211.k_own.v_own, bf16[512,2048]{1,0:T(8,128)(2,1)} %get-tuple-element.211.k_own.v_own, ...), custom_call_target="tpu_custom_call" | custom-call | flops 3221225472 | bytes 10485760 | tf_op jit(solution)/shard_map/self_fwd/pallas_call | solution.py:178
  309.2 11.8 %cross_fwd.1 = (bf16[512,1024]{1,0:T(8,128)(2,1)}, f32[8,8,512]{2,1,0:T(8,128)}) custom-call(bf16[512,1024]{1,0:T(8,128)(2,1)} %get-tuple-element.215.q, bf16[384,2048]{1,0:T(8,128)(2,1)} %shard_map.325.k.v, bf16[384,2048]{1,0:T(8,128)(2,1)} %shard_map.325.k.v), custom_call_target="tpu_custom_call" | custom-call | flops 1610612736 | bytes 4194304 | tf_op jit(solution)/shard_map/cross_fwd/pallas_call | solution.py:270
  329.7 18.8 %shard_map.327 = (bf16[3,512,1408]{2,1,0:T(8,128)(2,1)}, f32[512,1024]{1,0:T(8,128)}, f32[512,1024]{1,0:T(8,128)}) custom-call(bf16[4,528,128]{2,1,0:T(8,128)(2,1)} %bitcast.216, bf16[4,528,128]{2,1,0:T(8,128)(2,1)} %collective-permute-done.20.refs_1_, bf16[4,528,128]{2,1,0:T(8,128)(2,1)} %collective-permute-done.24.refs_2_, ...), custom_call_target="tpu_custom_call" | custom-call | flops 8858370048 | bytes 14942208 | tf_op jit(solution)/shard_map/pallas_call | solution.py:374
  355.8 18.7 %shard_map.330 = (bf16[3,512,1408]{2,1,0:T(8,128)(2,1)}, bf16[512,1024]{1,0:T(8,128)(2,1)}, f32[512,1024]{1,0:T(8,128)}) custom-call(bf16[4,528,128]{2,1,0:T(8,128)(2,1)} %bitcast.207, bf16[4,528,128]{2,1,0:T(8,128)(2,1)} %collective-permute-done.30.refs_1_, bf16[4,528,128]{2,1,0:T(8,128)(2,1)} %copy-done.73, ...), custom_call_target="tpu_custom_call" | custom-call | flops 8858370048 | bytes 14942208 | tf_op jit(solution)/shard_map/pallas_call | solution.py:374
  382.5 7.1 shard_map.333
  389.6 13.8 %cross_bwd.1 = (bf16[512,1024]{1,0:T(8,128)(2,1)}, bf16[384,2048]{1,0:T(8,128)(2,1)}) custom-call(bf16[512,1024]{1,0:T(8,128)(2,1)} %get-tuple-element.215.q, bf16[384,2048]{1,0:T(8,128)(2,1)} %shard_map.325.k.v, bf16[384,2048]{1,0:T(8,128)(2,1)} %shard_map.325.k.v, bf16[512,1024]{1,0:T(8,128)(2,1)} %get-tuple-element.261.grad, ...), custom_call_target="tpu_custom_call" | custom-call | flops 4026531840 | bytes 6291456 | tf_op jit(solution)/shard_map/cross_bwd/pallas_call | solution.py:289
  404.8 7.9 %shard_map.329 = (bf16[2,4,528,128]{3,2,1,0:T(8,128)(2,1)}, bf16[2,4,528,128]{3,2,1,0:T(8,128)(2,1)}, bf16[2,4,528,128]{3,2,1,0:T(8,128)(2,1)}, bf16[2,4,528,128]{3,2,1,0:T(8,128)(2,1)}) custom-call(bf16[3,512,1408]{2,1,0:T(8,128)(2,1)} %get-tuple-element.229.refs_0_, bf16[512,1024]{1,0:T(8,128)(2,1)} %get-tuple-element.223.refs_16_.refs_1_, ...), custom_call_target="tpu_custom_call" | custom-call | flops 2214592512 | bytes 12976128 | tf_op jit(solution)/shard_map/pallas_call | solution.py:542
  423.5 8.0 %shard_map.332 = (bf16[2,4,528,128]{3,2,1,0:T(8,128)(2,1)}, bf16[2,4,528,128]{3,2,1,0:T(8,128)(2,1)}, bf16[2,4,528,128]{3,2,1,0:T(8,128)(2,1)}, bf16[2,4,528,128]{3,2,1,0:T(8,128)(2,1)}) custom-call(bf16[3,512,1408]{2,1,0:T(8,128)(2,1)} %get-tuple-element.246.refs_0_, bf16[512,1024]{1,0:T(8,128)(2,1)} %get-tuple-element.223.refs_16_.refs_1_, ...), custom_call_target="tpu_custom_call" | custom-call | flops 2214592512 | bytes 12976128 | tf_op jit(solution)/shard_map/pallas_call | solution.py:542
  431.4 7.4 %collective-permute-done.62.refs_1_ = bf16[2,4,528,128]{3,2,1,0:T(8,128)(2,1)S(1)} collective-permute-done((bf16[2,4,528,128]{3,2,1,0:T(8,128)(2,1)}, bf16[2,4,528,128]{3,2,1,0:T(8,128)(2,1)S(1)}, u32[]{:S(2)}, u32[]{:S(2)}) %collective-permute-start.62) | collective-permute-done | bytes 1081376 | tf_op jit(solution)/shard_map/ppermute | solution.py:1228
  453.0 8.8 %shard_map.338 = (f32[512,1024]{1,0:T(8,128)}, bf16[512,1024]{1,0:T(8,128)(2,1)}, bf16[512,1024]{1,0:T(8,128)(2,1)}, f32[1,1024]{1,0:T(1,128)}) custom-call(bf16[4,512,128]{2,1,0:T(8,128)(2,1)} %bitcast.191, bf16[4,512,128]{2,1,0:T(8,128)(2,1)} %copy-done.10, bf16[4,512,128]{2,1,0:T(8,128)(2,1)} %collective-permute-done.11.refs_10_.refs_2_, ...), custom_call_target="tpu_custom_call" | custom-call | flops 2147483648 | bytes 13635584 | tf_op jit(solution)/shard_map/pallas_call | solution.py:374
  466.8 29.1 %self_bwd.1 = (bf16[512,1024]{1,0:T(8,128)(2,1)}, bf16[512,2048]{1,0:T(8,128)(2,1)}, bf16[512,2048]{1,0:T(8,128)(2,1)}, f32[8,64,512]{2,1,0:T(8,128)}) custom-call(s32[1]{0:T(128)} %bitcast.29.core, bf16[512,1024]{1,0:T(8,128)(2,1)} %shard_map.323.q, bf16[512,2048]{1,0:T(8,128)(2,1)} %get-tuple-element.211.k_own.v_own, ...), custom_call_target="tpu_custom_call" | custom-call | flops 8053063680 | bytes 20971520 | tf_op jit(solution)/shard_map/self_bwd/pallas_call | solution.py:200
  572.4 10.5 %shard_map.339 = (bf16[512,1024]{1,0:T(8,128)(2,1)}, f32[1,1024]{1,0:T(1,128)}) custom-call(bf16[4,512,128]{2,1,0:T(8,128)(2,1)} %bitcast.184, bf16[4,512,128]{2,1,0:T(8,128)(2,1)} %copy-done.6, bf16[4,512,128]{2,1,0:T(8,128)(2,1)} %copy-done.4, bf16[4,512,128]{2,1,0:T(8,128)(2,1)} %copy-done.7, bf16[4,512,128]{2,1,0:T(8,128)(2,1)} %copy-done.5, ...), custom_call_target="tpu_custom_call" | custom-call | flops 3221225472 | bytes 14684160 | tf_op jit(solution)/shard_map/pallas_call | solution.py:374
  630.5 27.6 %collective-permute-start.83 = (bf16[128,1024]{1,0:T(8,128)(2,1)}, bf16[128,1024]{1,0:T(8,128)(2,1)}, u32[]{:S(2)}, u32[]{:S(2)}) collective-permute-start(bf16[128,1024]{1,0:T(8,128)(2,1)} %get-tuple-element.273), channel_id=1, source_target_pairs={{0,6},{1,7},{2,0},{3,1},{4,14},{5,15},{6,8},{7,9},{8,2},{9,3},{10,... | collective-permute-start | bytes 786440 | tf_op jit(solution)/shard_map/ppermute | solution.py:1228
  (579 shorter events, 392.2 us)
Async XLA Ops:
  11.9 61.3 %all-gather.11.cloned.1.call-start = ((), (), s32[]{:S(2)}) async-start(), calls=%async_computation.9 | async-start | bytes 1310720 | tf_op jit(solution)/shard_map/all_gather | solution.py:1325
  16.5 94.8 %all-gather.13.cloned.1.call-start = ((), (), s32[]{:S(2)}) async-start(), calls=%async_computation.10 | async-start | bytes 1351680 | tf_op jit(solution)/shard_map/all_gather | solution.py:1325
  19.1 148.5 %all-gather.15.cloned.1.call-start = ((), (), s32[]{:S(2)}) async-start(), calls=%async_computation.11 | async-start | bytes 1351680 | tf_op jit(solution)/shard_map/all_gather | solution.py:1325
  19.9 568.3 %reduce-scatter.7.cloned.1.call-start = ((), (), s32[]{:S(2)}) async-start(), calls=%async_computation.5 | async-start | bytes 1351680 | tf_op jit(solution)/shard_map/reduce_scatter | solution.py:1337
  230.2 47.8 %collective-permute-start.52 = (bf16[512,2048]{1,0:T(8,128)(2,1)}, bf16[512,2048]{1,0:T(8,128)(2,1)}, u32[]{:S(2)}, u32[]{:S(2)}) collective-permute-start(bf16[512,2048]{1,0:T(8,128)(2,1)} %get-tuple-element.211.k_own.v_own), channel_id=1, source_target_pairs={{0,8},{1,9},{2,10},{3,11},{4,12},{5,13},{6,14},{7,15},{8,0},{9,1},... | collective-permute-start | bytes 6291464 | tf_op jit(solution)/shard_map/ppermute | solution.py:1228
  276.9 50.2 %collective-permute-start.38 = (bf16[4,528,128]{2,1,0:T(8,128)(2,1)}, bf16[4,528,128]{2,1,0:T(8,128)(2,1)}, u32[]{:S(2)}, u32[]{:S(2)}) collective-permute-start(bf16[4,528,128]{2,1,0:T(8,128)(2,1)} %collective-permute-done.24.refs_2_), channel_id=1, source_target_pairs={{0,8},{1,9},{2,10},{3,11},{4,12},{5,13},{6,14},{7,15},{8,0},{9,1},... | collective-permute-start | bytes 1622024 | tf_op jit(solution)/shard_map/ppermute | solution.py:1228
  277.5 50.1 %collective-permute-start.39 = (bf16[4,528,128]{2,1,0:T(8,128)(2,1)}, bf16[4,528,128]{2,1,0:T(8,128)(2,1)}, u32[]{:S(2)}, u32[]{:S(2)}) collective-permute-start(bf16[4,528,128]{2,1,0:T(8,128)(2,1)} %collective-permute-done.25.refs_3_), channel_id=1, source_target_pairs={{0,8},{1,9},{2,10},{3,11},{4,12},{5,13},{6,14},{7,15},{8,0},{9,1},... | collective-permute-start | bytes 1622024 | tf_op jit(solution)/shard_map/ppermute | solution.py:1228
  277.6 50.1 %collective-permute-start.40 = (bf16[4,528,128]{2,1,0:T(8,128)(2,1)}, bf16[4,528,128]{2,1,0:T(8,128)(2,1)S(1)}, u32[]{:S(2)}, u32[]{:S(2)}) collective-permute-start(bf16[4,528,128]{2,1,0:T(8,128)(2,1)} %collective-permute-done.26.refs_9_), channel_id=1, source_target_pairs={{0,8},{1,9},{2,10},{3,11},{4,12},{5,13},{6,14},{7,15},{8,0},{9,1},... | collective-permute-start | bytes 1622024 | tf_op jit(solution)/shard_map/ppermute | solution.py:1228
  278.0 50.1 %collective-permute-start.41 = (bf16[4,528,128]{2,1,0:T(8,128)(2,1)}, bf16[4,528,128]{2,1,0:T(8,128)(2,1)}, u32[]{:S(2)}, u32[]{:S(2)}) collective-permute-start(bf16[4,528,128]{2,1,0:T(8,128)(2,1)} %collective-permute-done.27.refs_11_), channel_id=1, source_target_pairs={{0,8},{1,9},{2,10},{3,11},{4,12},{5,13},{6,14},{7,15},{8,0},{9,1},... | collective-permute-start | bytes 1622024 | tf_op jit(solution)/shard_map/ppermute | solution.py:1228
  301.3 54.0 %collective-permute-start.70 = (bf16[4,528,128]{2,1,0:T(8,128)(2,1)}, bf16[4,528,128]{2,1,0:T(8,128)(2,1)}, u32[]{:S(2)}, u32[]{:S(2)}) collective-permute-start(bf16[4,528,128]{2,1,0:T(8,128)(2,1)} %copy-done.73), channel_id=1, source_target_pairs={{0,8},{1,9},{2,10},{3,11},{4,12},{5,13},{6,14},{7,15},{8,0},{9,1},... | collective-permute-start | bytes 1622024 | tf_op jit(solution)/shard_map/ppermute | solution.py:1228
  355.2 48.2 %collective-permute-start.60 = (bf16[4,4,528,128]{3,2,1,0:T(8,128)(2,1)}, bf16[4,4,528,128]{3,2,1,0:T(8,128)(2,1)S(1)}, u32[]{:S(2)}, u32[]{:S(2)}) collective-permute-start(bf16[4,4,528,128]{3,2,1,0:T(8,128)(2,1)} %get-tuple-element.230), channel_id=1, source_target_pairs={{0,8},{1,9},{2,10},{3,11},{4,12},{5,13},{6,14},{7,15},{8,0},{9,1},... | collective-permute-start | bytes 6488072 | tf_op jit(solution)/shard_map/ppermute | solution.py:1228
  355.3 48.1 %collective-permute-start.61 = (bf16[4,4,528,128]{3,2,1,0:T(8,128)(2,1)}, bf16[4,4,528,128]{3,2,1,0:T(8,128)(2,1)}, u32[]{:S(2)}, u32[]{:S(2)}) collective-permute-start(bf16[4,4,528,128]{3,2,1,0:T(8,128)(2,1)} %get-tuple-element.231), channel_id=1, source_target_pairs={{0,8},{1,9},{2,10},{3,11},{4,12},{5,13},{6,14},{7,15},{8,0},{9,1},... | collective-permute-start | bytes 6488072 | tf_op jit(solution)/shard_map/ppermute | solution.py:1228
  381.2 41.7 %collective-permute-start.74 = (bf16[4,4,528,128]{3,2,1,0:T(8,128)(2,1)}, bf16[4,4,528,128]{3,2,1,0:T(8,128)(2,1)}, u32[]{:S(2)}, u32[]{:S(2)}) collective-permute-start(bf16[4,4,528,128]{3,2,1,0:T(8,128)(2,1)} %get-tuple-element.247), channel_id=1, source_target_pairs={{0,8},{1,9},{2,10},{3,11},{4,12},{5,13},{6,14},{7,15},{8,0},{9,1},... | collective-permute-start | bytes 6488072 | tf_op jit(solution)/shard_map/ppermute | solution.py:1228
  381.3 42.2 %collective-permute-start.75 = (bf16[4,4,528,128]{3,2,1,0:T(8,128)(2,1)}, bf16[4,4,528,128]{3,2,1,0:T(8,128)(2,1)}, u32[]{:S(2)}, u32[]{:S(2)}) collective-permute-start(bf16[4,4,528,128]{3,2,1,0:T(8,128)(2,1)} %get-tuple-element.248), channel_id=1, source_target_pairs={{0,8},{1,9},{2,10},{3,11},{4,12},{5,13},{6,14},{7,15},{8,0},{9,1},... | collective-permute-start | bytes 6488072 | tf_op jit(solution)/shard_map/ppermute | solution.py:1228
  422.9 89.8 %collective-permute-start.80 = (bf16[4,4,512,128]{3,2,1,0:T(8,128)(2,1)}, bf16[4,4,512,128]{3,2,1,0:T(8,128)(2,1)}, u32[]{:S(2)}, u32[]{:S(2)}) collective-permute-start(bf16[4,4,512,128]{3,2,1,0:T(8,128)(2,1)} %shard_map.336), channel_id=1, source_target_pairs={{0,8},{1,9},{2,10},{3,11},{4,12},{5,13},{6,14},{7,15},{8,0},{9,1},... | collective-permute-start | bytes 6291464 | tf_op jit(solution)/shard_map/ppermute | solution.py:1228
  451.1 66.5 %collective-permute-start.79 = (bf16[4,4,512,128]{3,2,1,0:T(8,128)(2,1)}, bf16[4,4,512,128]{3,2,1,0:T(8,128)(2,1)}, u32[]{:S(2)}, u32[]{:S(2)}) collective-permute-start(bf16[4,4,512,128]{3,2,1,0:T(8,128)(2,1)} %shard_map.334), channel_id=1, source_target_pairs={{0,8},{1,9},{2,10},{3,11},{4,12},{5,13},{6,14},{7,15},{8,0},{9,1},... | collective-permute-start | bytes 6291464 | tf_op jit(solution)/shard_map/ppermute | solution.py:1228
  466.7 197.3 %reduce-scatter.5.cloned.1.call-start = ((), (), s32[]{:S(2)}) async-start(), calls=%async_computation.4 | async-start | bytes 1351680 | tf_op jit(solution)/shard_map/reduce_scatter | solution.py:1337
  495.9 68.4 %collective-permute-start.85 = (bf16[512,2048]{1,0:T(8,128)(2,1)}, bf16[512,2048]{1,0:T(8,128)(2,1)}, u32[]{:S(2)}, u32[]{:S(2)}) collective-permute-start(bf16[512,2048]{1,0:T(8,128)(2,1)} %get-tuple-element.280), channel_id=1, source_target_pairs={{0,8},{1,9},{2,10},{3,11},{4,12},{5,13},{6,14},{7,15},{8,0},{9,1},... | collective-permute-start | bytes 6291464 | tf_op jit(solution)/shard_map/ppermute | solution.py:1228
  512.7 86.7 %collective-permute-start.96 = (bf16[4,4,512,128]{3,2,1,0:T(8,128)(2,1)}, bf16[4,4,512,128]{3,2,1,0:T(8,128)(2,1)}, u32[]{:S(2)}, u32[]{:S(2)}) collective-permute-start(bf16[4,4,512,128]{3,2,1,0:T(8,128)(2,1)} %shard_map.343), channel_id=1, source_target_pairs={{0,8},{1,9},{2,10},{3,11},{4,12},{5,13},{6,14},{7,15},{8,0},{9,1},... | collective-permute-start | bytes 6291464 | tf_op jit(solution)/shard_map/ppermute | solution.py:1228
  546.7 129.6 %reduce-scatter.9.cloned.1.call-start = ((), (), s32[]{:S(2)}) async-start(), calls=%async_computation.6 | async-start | bytes 1310720 | tf_op jit(solution)/shard_map/reduce_scatter | solution.py:1337
  572.4 47.2 %collective-permute-start.94 = (bf16[4,4,512,128]{3,2,1,0:T(8,128)(2,1)}, bf16[4,4,512,128]{3,2,1,0:T(8,128)(2,1)}, u32[]{:S(2)}, u32[]{:S(2)}) collective-permute-start(bf16[4,4,512,128]{3,2,1,0:T(8,128)(2,1)} %shard_map.341), channel_id=1, source_target_pairs={{0,8},{1,9},{2,10},{3,11},{4,12},{5,13},{6,14},{7,15},{8,0},{9,1},... | collective-permute-start | bytes 6291464 | tf_op jit(solution)/shard_map/ppermute | solution.py:1228
  615.5 44.8 %collective-permute-start.97 = (bf16[2,4,512,128]{3,2,1,0:T(8,128)(2,1)}, bf16[2,4,512,128]{3,2,1,0:T(8,128)(2,1)S(1)}, u32[]{:S(2)}, u32[]{:S(2)}) collective-permute-start(bf16[2,4,512,128]{3,2,1,0:T(8,128)(2,1)} %get-tuple-element.290), channel_id=1, source_target_pairs={{0,16},{1,17},{2,18},{3,19},{4,20},{5,21},{6,22},{7,23},{8,24},{9,... | collective-permute-start | bytes 3145736 | tf_op jit(solution)/shard_map/ppermute | solution.py:1228
  619.6 98.3 %reduce-scatter.11.cloned.1.call-start = ((), (), s32[]{:S(2)}) async-start(), calls=%async_computation.7 | async-start | bytes 1310720 | tf_op jit(solution)/shard_map/reduce_scatter | solution.py:1337
  630.5 44.2 %collective-permute-start.83 = (bf16[128,1024]{1,0:T(8,128)(2,1)}, bf16[128,1024]{1,0:T(8,128)(2,1)}, u32[]{:S(2)}, u32[]{:S(2)}) collective-permute-start(bf16[128,1024]{1,0:T(8,128)(2,1)} %get-tuple-element.273), channel_id=1, source_target_pairs={{0,6},{1,7},{2,0},{3,1},{4,14},{5,15},{6,8},{7,9},{8,2},{9,3},{10,... | collective-permute-start | bytes 786440 | tf_op jit(solution)/shard_map/ppermute | solution.py:1228
  (175 other events, 3346.9 us)
Sparse Core Ops, SparseCore 0:
  12.1 30.6 all-gather.8
  44.9 27.3 all-gather.10
  74.5 28.1 all-gather.12
  104.6 39.2 all-gather.14
  466.8 31.6 reduce-scatter.6
  546.8 31.0 reduce-scatter.4
  619.7 27.6 reduce-scatter.8
  688.7 29.1 reduce-scatter.10
where the time goes:
time: 741 us; the launch traced here: 730 us
  Pallas kernels  280 us (38%)
  waiting for transfers between devices  179 us (24%)
  starting transfers between devices  156 us (21%)
  local copies, waits for them, and re-layouts  62.7 us (8%)
  other arithmetic  33.5 us (5%)
  between operations  16.2 us (2%)
    ppermute x111, waiting for transfers between devices, move(): return lax.ppermute(x, AXES, pairs)  157 us
    ppermute x111, starting transfers between devices, move(): return lax.ppermute(x, AXES, pairs)  150 us
    pallas_call x11, Pallas kernels, staged(): pl.pallas_call(partial(staged_kernel, body, plan, len(flat), len(tiled),...  101 us
    pallas_call x12, Pallas kernels, weight_grads(): pl.pallas_call(partial(grads_kernel, size, ways, kept, two), grid=(count,...  64.5 us
    unnamed x172, local copies, waits for them, and re-layouts  31.1 us
    pallas_call x1, Pallas kernels, self_backward(): pl.pallas_call(self_backward_kernel, grid_spec=pltpu.PrefetchScalarGridSp...  29.1 us
    pallas_call x1, Pallas kernels, self_forward(): pl.pallas_call(self_forward_kernel, grid_spec=pltpu.PrefetchScalarGridSpe...  23.2 us
    all_gather x4, waiting for transfers between devices, spread(): both = lax.all_gather(jnp.stack(pieces), TP, axis=1)  19 us
  transfers between devices with their start and end apart: 121, of which 38 were waited for; matrix products, arithmetic and copies ran while one was open for 11% of the time, Pallas kernels for 38%

commit v1 on v0

--- a/solution.py
+++ b/solution.py
@@ -44,12 +44,13 @@
     return jnp.where(left, first, second)
 
 
-def row_softmax(tiles):
-    peak = jnp.max(tiles[0], axis=1, keepdims=True)
+def col_softmax(tiles):
+    peak = tiles[0]
     for tile in tiles[1:]:
-        peak = jnp.maximum(peak, jnp.max(tile, axis=1, keepdims=True))
+        peak = jnp.maximum(peak, tile)
+    peak = jnp.max(peak, axis=0, keepdims=True)
     exps = [jnp.exp(tile - peak) for tile in tiles]
-    total = jnp.sum(reduce_add(exps), axis=1, keepdims=True)
+    total = jnp.sum(reduce_add(exps), axis=0, keepdims=True)
     scale = 1.0 / total
     return [(e * scale).astype(BF) for e in exps], peak + jnp.log(total)
 
@@ -61,12 +62,22 @@
     return out
 
 
+def pick_late(swapped, first, second):
+    return jnp.where(swapped, first, second)
+
+
 def self_forward_kernel(core, q, k_own, v_own, k_far, v_far, lines, mask, out, logs):
     half = q.shape[0] // 2
     left = lax.broadcasted_iota(jnp.int32, (1, q.shape[1]), 1) < q.shape[1] // 2
     swapped = core[0] == 1
     a, b = slice(0, half), slice(half, 2 * half)
-    outs, totals = [], []
+    low = -3.0e38
+    k_late = pick_late(swapped, k_far[a, :], k_far[b, :])
+    v_late = pick_late(swapped, v_far[a, :], v_far[b, :])
+    mask_late = pick_late(
+        swapped, mask[2 * half : 3 * half, a], mask[3 * half : 4 * half, b]
+    )
+    outs = []
     for head in range(2):
         keep = left if head == 0 else jnp.logical_not(left)
         qh = jnp.where(keep, q[...], jnp.zeros((), BF))
@@ -74,36 +85,41 @@
         next_tile = toeplitz(lines[0, 2 * head + 1 : 2 * head + 2, :], half)
         far = lines[0, 4 + head : 5 + head, :half]
         qa, qb = qh[a], qh[b]
-        ka, kb, xa, xb = k_own[a, :], k_own[b, :], k_far[a, :], k_far[b, :]
-        pa, la = row_softmax(
-            [
-                nt(qa, ka) + near + mask[a, 0:half],
-                nt(qa, xa) + next_tile + mask[a, 2 * half : 3 * half],
-            ]
-        )
-        oa = nn(pa[0], v_own[a, :]) + nn(pa[1], v_far[a, :])
-        pb, lb = row_softmax(
-            [
-                nt(qb, ka) + jnp.where(swapped, next_tile, far) + mask[b, 0:half],
-                nt(qb, kb) + near + mask[b, half : 2 * half],
-                nt(qb, xa) + far + mask[b, 2 * half : 3 * half],
-                nt(qb, xb) + next_tile + mask[b, 3 * half : 4 * half],
-            ]
-        )
-        ob = (
-            nn(pb[0], v_own[a, :])
-            + nn(pb[1], v_own[b, :])
-            + nn(pb[2], v_far[a, :])
-            + nn(pb[3], v_far[b, :])
-        )
+        ka, kb, xa = k_own[a, :], k_own[b, :], k_far[a, :]
+        tiles_a = [nt(ka, qa) + near + mask[0:half, a]]
+        tiles_b = [
+            nt(ka, qb) + jnp.where(swapped, next_tile, far) + mask[0:half, b],
+            nt(kb, qb) + near + mask[half : 2 * half, b],
+            nt(xa, qb) + far + mask[2 * half : 3 * half, b],
+        ]
+        late = nt(k_late, pick_late(swapped, qa, qb)) + next_tile + mask_late
+        late_peak = jnp.max(late, axis=0, keepdims=True)
+        peak_a = jnp.max(tiles_a[0], axis=0, keepdims=True)
+        peak_b = jnp.max(
+            jnp.maximum(jnp.maximum(tiles_b[0], tiles_b[1]), tiles_b[2]), axis=0, keepdims=True
+        )
+        peak_a = jnp.maximum(peak_a, pick_late(swapped, late_peak, low))
+        peak_b = jnp.maximum(peak_b, pick_late(swapped, low, late_peak))
+        exps_a = [jnp.exp(tile - peak_a) for tile in tiles_a]
+        exps_b = [jnp.exp(tile - peak_b) for tile in tiles_b]
+        exp_late = jnp.exp(late - pick_late(swapped, peak_a, peak_b))
+        sum_late = jnp.sum(exp_late, axis=0, keepdims=True)
+        total_a = jnp.sum(exps_a[0], axis=0, keepdims=True) + pick_late(swapped, sum_late, 0.0)
+        total_b = jnp.sum(reduce_add(exps_b), axis=0, keepdims=True) + pick_late(
+            swapped, 0.0, sum_late
+        )
+        scale_a, scale_b = 1.0 / total_a, 1.0 / total_b
+        out_late = tn((exp_late * pick_late(swapped, scale_a, scale_b)).astype(BF), v_late)
+        oa = tn((exps_a[0] * scale_a).astype(BF), v_own[a, :])
+        pb = [(e * scale_b).astype(BF) for e in exps_b]
+        ob = tn(pb[0], v_own[a, :]) + tn(pb[1], v_own[b, :]) + tn(pb[2], v_far[a, :])
+        oa = oa + pick_late(swapped, out_late, 0.0)
+        ob = ob + pick_late(swapped, 0.0, out_late)
         outs.append((oa, ob))
-        totals.append((la, lb))
+        logs[0, head : head + 1, a] = peak_a + jnp.log(total_a)
+        logs[0, head : head + 1, b] = peak_b + jnp.log(total_b)
     out[a, :] = lane_pick(outs[0][0], outs[1][0], left).astype(BF)
     out[b, :] = lane_pick(outs[0][1], outs[1][1], left).astype(BF)
-    for at, piece in ((0, a), (1, b)):
-        turned = lane_pick(totals[0][at], totals[1][at], left).T
-        logs[0, 0:1, piece] = turned[0:1, :]
-        logs[0, 1:2, piece] = turned[q.shape[1] // 2 : q.shape[1] // 2 + 1, :]
 
 
 def self_backward_kernel(
@@ -114,52 +130,80 @@
     left = lax.broadcasted_iota(jnp.int32, (1, q.shape[1]), 1) < q.shape[1] // 2
     swapped = core[0] == 1
     a, b = slice(0, half), slice(half, 2 * half)
-    keys = {"oa": (k_own, v_own, a, 0), "ob": (k_own, v_own, b, 1), "xa": (k_far, v_far, a, 2), "xb": (k_far, v_far, b, 3)}
-    dk, dv, dqs = {}, {}, [None, None]
+    zero = jnp.zeros((), BF)
+    mask_late = pick_late(
+        swapped, mask[2 * half : 3 * half, a], mask[3 * half : 4 * half, b]
+    )
+    keys = {
+        "oa": (k_own[a, :], v_own[a, :]),
+        "ob": (k_own[b, :], v_own[b, :]),
+        "xa": (k_far[a, :], v_far[a, :]),
+        "x": (
+            pick_late(swapped, k_far[a, :], k_far[b, :]),
+            pick_late(swapped, v_far[a, :], v_far[b, :]),
+        ),
+    }
+    dk, dv, dqs = {}, {}, {}
+
+    def grow(store, name, value):
+        store[name] = value if name not in store else store[name] + value
+
     for head in range(2):
         keep = left if head == 0 else jnp.logical_not(left)
-        zero = jnp.zeros((), BF)
         qh = jnp.where(keep, q[...], zero)
         gh = jnp.where(keep, grad[...], zero)
         near = toeplitz(lines[0, 2 * head : 2 * head + 1, :], half)
         next_tile = toeplitz(lines[0, 2 * head + 1 : 2 * head + 2, :], half)
         far = lines[0, 4 + head : 5 + head, :half]
+        log_a, log_b = logs[0, head : head + 1, a], logs[0, head : head + 1, b]
+        queries = {"a": (qh[a], gh[a], log_a), "b": (qh[b], gh[b], log_b)}
+        queries["x"] = tuple(pick_late(swapped, u, v) for u, v in zip(queries["a"], queries["b"]))
+        plan = (
+            ("a", "oa", near, mask[0:half, a]),
+            ("b", "oa", jnp.where(swapped, next_tile, far), mask[0:half, b]),
+            ("b", "ob", near, mask[half : 2 * half, b]),
+            ("b", "xa", far, mask[2 * half : 3 * half, b]),
+            ("x", "x", next_tile, mask_late),
+        )
+        probs, dots, sums_of = [], [], {}
+        for side, name, bias, hide in plan:
+            qp, gp, total = queries[side]
+            k, v = keys[name]
+            p = jnp.exp(nt(k, qp) + bias + hide - total)
+            d = nt(v, gp)
+            probs.append(p)
+            dots.append(d)
+            grow(sums_of, side, p * d)
+        delta = {side: jnp.sum(v, axis=0, keepdims=True) for side, v in sums_of.items()}
+        delta_a = delta["a"] + pick_late(swapped, delta["x"], 0.0)
+        delta_b = delta["b"] + pick_late(swapped, 0.0, delta["x"])
+        delta = {"a": delta_a, "b": delta_b, "x": pick_late(swapped, delta_a, delta_b)}
         held = {}
-        for at, piece, plan in (
-            (0, a, (("oa", near), ("xa", next_tile))),
-            (1, b, (("oa", jnp.where(swapped, next_tile, far)), ("ob", near), ("xa", far), ("xb", next_tile))),
-        ):
-            qp, gp = qh[piece], gh[piece]
-            total = logs[0, head : head + 1, piece]
-            probs, dots = [], []
-            for name, bias in plan:
-                k, v, rows, slot = keys[name]
-                score = nt(k[rows, :], qp) + bias + mask[slot * half : (slot + 1) * half, piece]
-                probs.append(jnp.exp(score - total))
-                dots.append(nt(v[rows, :], gp))
-            delta = jnp.sum(reduce_add([p * d for p, d in zip(probs, dots)]), axis=0, keepdims=True)
-            for (name, _), p, d in zip(plan, probs, dots):
-                k, v, rows, slot = keys[name]
-                ds = p * (d - delta)
-                held[at, name] = ds
-                low = ds.astype(BF)
-                dvp, dkp = nn(p.astype(BF), gp), nn(low, qp)
-                dv[name] = dvp if name not in dv else dv[name] + dvp
-                dk[name] = dkp if name not in dk else dk[name] + dkp
-                dqp = tn(low, jnp.where(keep, k[rows, :], zero))
-                dqs[at] = dqp if dqs[at] is None else dqs[at] + dqp
+        for (side, name, _, _), p, d in zip(plan, probs, dots):
+            qp, gp, _ = queries[side]
+            k, _ = keys[name]
+            ds = p * (d - delta[side])
+            held[side, name] = ds
+            low = ds.astype(BF)
+            grow(dv, name, nn(p.astype(BF), gp))
+            grow(dk, name, nn(low, qp))
+            grow(dqs, side, tn(low, jnp.where(keep, k, zero)))
         base = 32 * head
-        sums[0, base : base + 8, :] = diagonals(held[0, "oa"] + held[1, "ob"], half)
-        sums[0, base + 8 : base + 16, :] = diagonals(held[0, "xa"] + held[1, "xb"], half)
-        sums[0, base + 16 : base + 24, :] = diagonals(held[1, "oa"], half)
-        rest = reduce_add([held[1, "xa"][at : at + 8, :] for at in range(0, half, 8)])
+        sums[0, base : base + 8, :] = diagonals(held["a", "oa"] + held["b", "ob"], half)
+        sums[0, base + 8 : base + 16, :] = diagonals(held["x", "x"], half)
+        sums[0, base + 16 : base + 24, :] = diagonals(held["b", "oa"], half)
+        rest = reduce_add([held["b", "xa"][at : at + 8, :] for at in range(0, half, 8)])
         sums[0, base + 24 : base + 32, :] = jnp.concatenate([rest, jnp.zeros_like(rest)], axis=1)
-    dq[a, :] = dqs[0].astype(BF)
-    dq[b, :] = dqs[1].astype(BF)
+    dq[a, :] = (dqs["a"] + pick_late(swapped, dqs["x"], 0.0)).astype(BF)
+    dq[b, :] = (dqs["b"] + pick_late(swapped, 0.0, dqs["x"])).astype(BF)
     sub = pl.multiple_of(lax.rem(pl.program_id(0), 2) * 128, 128)
-    for name, ref, rows in (("oa", own_out, a), ("ob", own_out, b), ("xa", far_out, a), ("xb", far_out, b)):
-        ref[rows, pl.ds(sub, 128)] = dk[name].astype(BF)
-        ref[rows, pl.ds(sub + 256, 128)] = dv[name].astype(BF)
+    for at, grads in ((0, dk), (256, dv)):
+        own_out[a, pl.ds(sub + at, 128)] = grads["oa"].astype(BF)
+        own_out[b, pl.ds(sub + at, 128)] = grads["ob"].astype(BF)
+        far_out[a, pl.ds(sub + at, 128)] = (
+            grads["xa"] + pick_late(swapped, grads["x"], 0.0)
+        ).astype(BF)
+        far_out[b, pl.ds(sub + at, 128)] = pick_late(swapped, 0.0, grads["x"]).astype(BF)
 
 
 def self_specs(rows):
@@ -180,7 +224,7 @@
         grid_spec=pltpu.PrefetchScalarGridSpec(
             num_scalar_prefetch=1,
             grid=(pairs,),
-            in_specs=[qs, ks, vs, ks, vs, small, pl.BlockSpec((rows, 2 * rows), lambda p, c: (0, 0))],
+            in_specs=[qs, ks, vs, ks, vs, small, pl.BlockSpec((2 * rows, rows), lambda p, c: (0, 0))],
             out_specs=[qs, small],
         ),
         out_shape=(
@@ -218,17 +262,16 @@
 
 def cross_forward_kernel(q, k, v, out, logs):
     left = lax.broadcasted_iota(jnp.int32, (1, q.shape[1]), 1) < q.shape[1] // 2
-    outs, totals = [], []
-    for head in range(2):
-        keep = left if head == 0 else jnp.logical_not(left)
-        qh = jnp.where(keep, q[...], jnp.zeros((), BF))
-        p, total = row_softmax([nt(qh, k[...])])
-        outs.append(nn(p[0], v[...]))
-        totals.append(total)
-    out[...] = lane_pick(outs[0], outs[1], left).astype(BF)
-    turned = lane_pick(totals[0], totals[1], left).T
-    logs[0, 0:1, :] = turned[0:1, :]
-    logs[0, 1:2, :] = turned[q.shape[1] // 2 : q.shape[1] // 2 + 1, :]
+    for at in range(0, q.shape[0], 128):
+        piece = slice(at, at + 128)
+        outs = []
+        for head in range(2):
+            keep = left if head == 0 else jnp.logical_not(left)
+            qh = jnp.where(keep, q[piece, :], jnp.zeros((), BF))
+            p, total = col_softmax([nt(k[...], qh)])
+            outs.append(tn(p[0], v[...]))
+            logs[0, head : head + 1, piece] = total
+        out[piece, :] = lane_pick(outs[0], outs[1], left).astype(BF)
 
 
 def cross_backward_kernel(q, k, v, grad, logs, dq, out):
@@ -441,7 +484,7 @@
 
 
 def feed_body(first, weight, tiled, whole, outs):
-    n, g, before, grad_before = tiled
+    n, g, before, *grad_before = tiled
     sides_out, after_out, normed_out = outs
     gate = nt(n[...], weight(0))
     up = nt(n[...], weight(1))
@@ -458,7 +501,10 @@
     grad_up = (grad * act).astype(BF)
     sides_out[0] = grad_gate
     sides_out[1] = grad_up
-    normed_out[...] = grad_before[...] + nn(grad_gate, weight(0)) + nn(grad_up, weight(1))
+    grad_normed = nn(grad_gate, weight(0)) + nn(grad_up, weight(1))
+    for part in grad_before:
+        grad_normed = grad_normed + part[...]
+    normed_out[...] = grad_normed
 
 
 def turn_body(first, weight, tiled, whole, outs):
@@ -1410,22 +1456,20 @@
     came_table = [from_z(rel_table, step) for step in (1, 2, 3)]
     near_s, core_s0 = settle(near_s, core_s0)
     far_s, core_s1 = far_of(held_s, near_s), cores_of(near_s)
-    far_s, core_s1, held_c = settle(far_s, core_s1, held_c)
+    far_s, core_s1, held_c, low_cotangent = settle(far_s, core_s1, held_c, cotangent)
     core_s2 = far_cores(far_s)
     near_c, core_c0 = near_of(held_c), cores_of(held_c)
+    came_grad = send_rows(low_cotangent, place)
     near_c, core_c0, held_f1 = settle(near_c, core_c0, held_f1)
     far_c, core_c1 = far_of(held_c, near_c), cores_of(near_c)
     near_f1, core_f10 = near_of(held_f1), cores_of(held_f1)
-    far_c, core_c1, near_f1, core_f10, held_f2, low_cotangent = settle(
-        far_c, core_c1, near_f1, core_f10, held_f2, cotangent
+    far_c, core_c1, near_f1, core_f10, came_grad = settle(
+        far_c, core_c1, near_f1, core_f10, came_grad
     )
     core_c2 = far_cores(far_c)
     far_f1, core_f11 = far_of(held_f1, near_f1), cores_of(near_f1)
     near_f2, core_f20 = near_of(held_f2), cores_of(held_f2)
-    came_grad = send_rows(low_cotangent, place)
-    far_f1, core_f11, near_f2, core_f20, came_grad = settle(
-        far_f1, core_f11, near_f2, core_f20, came_grad
-    )
+    far_f1, core_f11, near_f2, core_f20 = settle(far_f1, core_f11, near_f2, core_f20)
     core_f12 = far_cores(far_f1)
     far_f2, core_f21 = far_of(held_f2, near_f2), cores_of(near_f2)
     far_f2, core_f21 = settle(far_f2, core_f21)
@@ -1470,7 +1514,7 @@
             [near[:, 0:1], after[:, 0:1], near[:, 1:2], after[:, 1:2], far, blank], axis=1
         )
 
-    lines_forward, lines_backward = kernel_lines(-1), kernel_lines(1)
+    lines = kernel_lines(1)
 
     quarter = jnp.arange(half, dtype=jnp.int32)
     spots = jnp.concatenate([quarter + half * n for n in (core, 3 - core, 1 - core, 2 + core)])
@@ -1484,7 +1528,6 @@
     def mask_of(query_at, key_at, query_seg, key_seg):
         return jnp.where((query_seg == key_seg) & (key_at <= query_at), 0.0, masked_score).astype(F32)
 
-    mask = mask_of(spots[:rows, None], spots[None, :], seg_spots[:rows, None], seg_spots[None, :])
     mask_t = mask_of(spots[None, :rows], spots[:, None], seg_spots[None, :rows], seg_spots[:, None])
 
     tall = min(256, rows)
@@ -1501,7 +1544,7 @@
     )
     kv_far = flip_core(kv_own)
     (queries,) = staged(nt_body, [w_q], [normed_self], [], [full(width)], tall, dot * width)
-    mixed, self_logs = self_forward(core_id, queries, kv_own, kv_far, lines_forward, mask)
+    mixed, self_logs = self_forward(core_id, queries, kv_own, kv_far, lines, mask_t)
     (cross_kv,) = staged(
         nt_body, [w_ckv], [states], [],
         [((states.shape[0], 2 * width), BF)], states.shape[0], dot * width,
@@ -1516,11 +1559,11 @@
         [full(width, F32), full(width)], tall, dot * width,
     )
     grad_low = gather_rows_call(spot, came_grad)
-    total, grad_normed = after_cross, jnp.zeros((rows, width), F32)
+    total, grad_normed = after_cross, []
     feed_sides, feed_over = [], []
     for chunk in (0, 1):
-        sides, total, grad_normed = staged(
-            feed_body, w_feed[chunk], [normed_ffn, grad_low, total, grad_normed], [],
+        sides, total, *grad_normed = staged(
+            feed_body, w_feed[chunk], [normed_ffn, grad_low, total, *grad_normed], [],
             [((3, rows, 8 * cut), BF), full(width, BF if chunk else F32), full(width, F32)],
             tall, dot * 6 * 8 * cut,
         )
@@ -1538,11 +1581,14 @@
     def second_stage(jobs, came):
         return [way[1](h) for way, h in zip(WAYS, near_sums(jobs[1::2], came))]
 
-    def finish(jobs, came, last):
-        return collect(far_sums(jobs[1::2], came, last))
+    def finish(jobs, came, last, earlier):
+        both = far_sums(jobs[1::2], came, last)
+        if earlier is not None:
+            both, earlier = settle(both, earlier)
+        return collect(both), earlier
 
     grad_mid, low_mid, grad_cross_mixed, gain_three = staged(
-        turn_body, [w_co], [after_cross, grad_normed, grad_low], [gain_ffn],
+        turn_body, [w_co], [after_cross, *grad_normed, grad_low], [gain_ffn],
         [full(width, F32), full(width), full(width), gain_out], tall, dot * width,
     )
     grad_cq, shared = cross_backward(cross_q, cross_kv, grad_cross_mixed, cross_logs)
@@ -1564,7 +1610,7 @@
         [((own_states, width), BF)], own_states, dot * width,
     )
     grad_q, kv_kept, kv_sent, sums = self_backward(
-        core_id, queries, kv_own, kv_far, grad_mixed, lines_backward, mask_t, self_logs
+        core_id, queries, kv_own, kv_far, grad_mixed, lines, mask_t, self_logs
     )
     grad_kv = kv_kept + flip_core(kv_sent)
     pair_s = (grad_q, mixed)
@@ -1591,19 +1637,21 @@
 
     jobs_f1 = feed_jobs(0)
     n1 = first_stage(jobs_f1)
-    n1, jobs_f2 = settle(n1, feed_jobs(1))
+    (n1,) = settle(n1)
+    jobs_f2 = feed_jobs(1)
     n2 = second_stage(jobs_f1, n1)
-    done_f1 = finish(jobs_f1, n1, n2)
+    done_f1, _ = finish(jobs_f1, n1, n2, None)
     n1 = first_stage(jobs_f2)
-    n1, result_slots, jobs_c = settle(n1, result_slots, cross_jobs())
+    n1, result_slots = settle(n1, result_slots)
+    jobs_c = cross_jobs()
     n2 = second_stage(jobs_f2, n1)
     back_result = send_back(result_slots)
-    done_f2 = finish(jobs_f2, n1, n2)
+    done_f2, done_f1 = finish(jobs_f2, n1, n2, done_f1)
     n1 = first_stage(jobs_c)
-    n1, done_f1 = settle(n1, done_f1)
+    (n1,) = settle(n1)
     jobs_s = self_jobs()
     n2 = second_stage(jobs_c, n1)
-    done_c = finish(jobs_c, n1, n2)
+    done_c, done_f2 = finish(jobs_c, n1, n2, done_f2)
     state_abs = from_relative(state_grad, place)
     state_cols = jnp.stack([state_abs[:, at * inner : (at + 1) * inner] for at in range(4)])
     got = [
@@ -1614,10 +1662,9 @@
         for step in range(4)
     ]
     n1 = first_stage(jobs_s)
-    n1, done_f2 = settle(n1, done_f2)
+    (n1,) = settle(n1)
     back_tokens = send_back(token_slots)
     n2 = second_stage(jobs_s, n1)
-    n2, done_c = settle(n2, done_c)
     sum_s = far_sums(jobs_s[1::2], n1, n2)
 
     inside = (signed[None, :] - jnp.arange(8, dtype=jnp.int32)[:, None]) % (2 * half)
@@ -1636,7 +1683,7 @@
     by_z = table_grad.reshape(-1, 4, heads)
     gain_parts = from_relative(jnp.concatenate([gain_one, gain_two, gain_three]), place)
     small = jnp.concatenate([gain_parts.reshape(-1), by_z.reshape(-1)]).reshape(-1, 128)
-    sum_s, small = settle(sum_s, small)
+    sum_s, small, done_c = settle(sum_s, small, done_c)
     done_s = collect(sum_s)
     for flip in (
         flip_core,

time: 741 us -> 721 us (0.973)
  starting transfers between devices: 156 us -> 101 us
  waiting for transfers between devices: 179 us -> 228 us
  Pallas kernels: 280 us -> 266 us
    ppermute x111, starting transfers between devices: 150 us -> 96.3 us  [move(): return lax.ppermute(x, AXES, pairs)]
    all_gather x4, waiting for transfers between devices: 19 us -> 57.4 us  [spread(): both = lax.all_gather(jnp.stack(pieces), TP, axis=1)]
    ppermute x111, waiting for transfers between devices: 157 us -> 168 us  [move(): return lax.ppermute(x, AXES, pairs)]
    unnamed x172 -> x162, local copies, waits for them, and re-layouts: 31.1 us -> 29.4 us
  transfers between devices with their start and end apart: 121 -> 121, of which waited for: 38 -> 40; matrix products, arithmetic and copies ran while one was open for 11% -> 11% of each run, Pallas kernels for 38% -> 37%
where the time goes in v1:
time: 721 us; the launch traced here: 711 us
  Pallas kernels  266 us (37%)
  waiting for transfers between devices  228 us (32%)
  starting transfers between devices  101 us (14%)
  local copies, waits for them, and re-layouts  63.5 us (9%)
  other arithmetic  32.8 us (5%)
  between operations  16.1 us (2%)
    ppermute x111, waiting for transfers between devices, move(): return lax.ppermute(x, AXES, pairs)  168 us
    pallas_call x11, Pallas kernels, staged(): pl.pallas_call(partial(staged_kernel, body, plan, len(flat), len(tiled),...  101 us
    ppermute x111, starting transfers between devices, move(): return lax.ppermute(x, AXES, pairs)  96.3 us
    pallas_call x12, Pallas kernels, weight_grads(): pl.pallas_call(partial(grads_kernel, size, ways, kept, two), grid=(count,...  65 us
    all_gather x4, waiting for transfers between devices, spread(): both = lax.all_gather(jnp.stack(pieces), TP, axis=1)  57.4 us
    unnamed x162, local copies, waits for them, and re-layouts  29.4 us
    pallas_call x1, Pallas kernels, self_backward(): pl.pallas_call(self_backward_kernel, grid_spec=pltpu.PrefetchScalarGridSp...  23.6 us
    pallas_call x1, Pallas kernels, self_forward(): pl.pallas_call(self_forward_kernel, grid_spec=pltpu.PrefetchScalarGridSpe...  17.3 us
  transfers between devices with their start and end apart: 121, of which 40 were waited for; matrix products, arithmetic and copies ran while one was open for 11% of the time, Pallas kernels for 37%

profile of v1, /device:TPU:0, one launch (start us, length us, event | category | flops | bytes accessed | tf_op | source)
XLA Modules:
  0.0 711.0 jit_solution(2146488776310566898)
XLA Ops:
  24.9 18.0 %all-gather.11.cloned.1.call-done = bf16[2,2048,128]{2,1,0:T(8,128)(2,1)} async-done(((bf16[2,512,128]{2,1,0:T(8,128)(2,1)}), bf16[2,2048,128]{2,1,0:T(8,128)(2,1)}) %all-gather.11.cloned.1.call-update) | async-done | bytes 1048592 | tf_op jit(solution)/shard_map/all_gather | solution.py:1371
  94.4 23.6 %all-gather.13.cloned.1.call-done = bf16[2,2048,128]{2,1,0:T(8,128)(2,1)} async-done(((bf16[2,512,128]{2,1,0:T(8,128)(2,1)}), bf16[2,2048,128]{2,1,0:T(8,128)(2,1)}) %all-gather.13.cloned.1.call-update) | async-done | bytes 1048592 | tf_op jit(solution)/shard_map/all_gather | solution.py:1371
  127.2 7.6 %collective-permute-done.10.refs_1_ = bf16[4,512,128]{2,1,0:T(8,128)(2,1)} collective-permute-done((bf16[4,512,128]{2,1,0:T(8,128)(2,1)}, bf16[4,512,128]{2,1,0:T(8,128)(2,1)}, u32[]{:S(2)}, u32[]{:S(2)}) %collective-permute-start.10) | collective-permute-done | bytes 524320 | tf_op jit(solution)/shard_map/ppermute | solution.py:1274
  143.6 15.8 %all-gather.15.cloned.1.call-done = bf16[2,2112,128]{2,1,0:T(8,128)(2,1)} async-done(((bf16[2,528,128]{2,1,0:T(8,128)(2,1)}), bf16[2,2112,128]{2,1,0:T(8,128)(2,1)}) %all-gather.15.cloned.1.call-update) | async-done | bytes 1081360 | tf_op jit(solution)/shard_map/all_gather | solution.py:1371
  166.4 9.0 %collective-permute-done.17.refs_9_.refs_1_ = bf16[4,512,128]{2,1,0:T(8,128)(2,1)S(1)} collective-permute-done((bf16[4,512,128]{2,1,0:T(8,128)(2,1)S(1)}, bf16[4,512,128]{2,1,0:T(8,128)(2,1)S(1)}, u32[]{:S(2)}, u32[]{:S(2)}) %collective-permute-start.17) | collective-permute-done | bytes 524320 | tf_op jit(solution)/shard_map/ppermute | solution.py:1274
  175.4 11.2 %collective-permute-done.18.refs_11_.refs_3_ = bf16[4,512,128]{2,1,0:T(8,128)(2,1)} collective-permute-done((bf16[4,512,128]{2,1,0:T(8,128)(2,1)S(1)}, bf16[4,512,128]{2,1,0:T(8,128)(2,1)}, u32[]{:S(2)}, u32[]{:S(2)}) %collective-permute-start.18) | collective-permute-done | bytes 524320 | tf_op jit(solution)/shard_map/ppermute | solution.py:1274
  213.6 7.4 %shard_map.322 = (bf16[512,1024]{1,0:T(8,128)(2,1)}, bf16[512,2048]{1,0:T(8,128)(2,1)}) custom-call(bf16[4,512,128]{2,1,0:T(8,128)(2,1)} %bitcast.10.refs_0_.refs_8_, bf16[4,512,128]{2,1,0:T(8,128)(2,1)} %copy-done.34, bf16[4,512,128]{2,1,0:T(8,128)(2,1)} %collective-permute-done.refs_2_.refs_10_, ...), custom_call_target="tpu_custom_call" | custom-call | flops 2147483648 | bytes 5246976 | tf_op jit(solution)/shard_map/pallas_call | solution.py:417
  228.4 7.7 %collective-permute-done.38.refs_2_ = bf16[4,528,128]{2,1,0:T(8,128)(2,1)} collective-permute-done((bf16[4,528,128]{2,1,0:T(8,128)(2,1)}, bf16[4,528,128]{2,1,0:T(8,128)(2,1)}, u32[]{:S(2)}, u32[]{:S(2)}) %collective-permute-start.38) | collective-permute-done | bytes 540704 | tf_op jit(solution)/shard_map/ppermute | solution.py:1274
  241.6 10.5 %collective-permute-done.39.refs_3_ = bf16[4,528,128]{2,1,0:T(8,128)(2,1)S(1)} collective-permute-done((bf16[4,528,128]{2,1,0:T(8,128)(2,1)}, bf16[4,528,128]{2,1,0:T(8,128)(2,1)S(1)}, u32[]{:S(2)}, u32[]{:S(2)}) %collective-permute-start.39) | collective-permute-done | bytes 540704 | tf_op jit(solution)/shard_map/ppermute | solution.py:1274
  269.9 17.3 %self_fwd.1 = (bf16[512,1024]{1,0:T(8,128)(2,1)}, f32[8,8,512]{2,1,0:T(8,128)}) custom-call(s32[1]{0:T(128)} %bitcast.29.core, bf16[512,1024]{1,0:T(8,128)(2,1)} %shard_map.323.q, bf16[512,2048]{1,0:T(8,128)(2,1)} %get-tuple-element.201.k_own.v_own, bf16[512,2048]{1,0:T(8,128)(2,1)} %get-tuple-element.201.k_own.v_own, ...), custom_call_target="tpu_custom_call" | custom-call | flops 3221225472 | bytes 10485760 | tf_op jit(solution)/shard_map/self_fwd/pallas_call | solution.py:222
  295.1 9.5 %cross_fwd.1 = (bf16[512,1024]{1,0:T(8,128)(2,1)}, f32[8,8,512]{2,1,0:T(8,128)}) custom-call(bf16[512,1024]{1,0:T(8,128)(2,1)} %get-tuple-element.205.q, bf16[384,2048]{1,0:T(8,128)(2,1)} %shard_map.325.k.v, bf16[384,2048]{1,0:T(8,128)(2,1)} %shard_map.325.k.v), custom_call_target="tpu_custom_call" | custom-call | flops 1610612736 | bytes 4194304 | tf_op jit(solution)/shard_map/cross_fwd/pallas_call | solution.py:313
  311.6 18.7 %shard_map.327 = (bf16[3,512,1408]{2,1,0:T(8,128)(2,1)}, f32[512,1024]{1,0:T(8,128)}, f32[512,1024]{1,0:T(8,128)}) custom-call(bf16[4,528,128]{2,1,0:T(8,128)(2,1)} %bitcast.203, bf16[4,528,128]{2,1,0:T(8,128)(2,1)} %collective-permute-done.21.refs_1_, bf16[4,528,128]{2,1,0:T(8,128)(2,1)} %collective-permute-done.14.refs_2_, ...), custom_call_target="tpu_custom_call" | custom-call | flops 8858370048 | bytes 12845056 | tf_op jit(solution)/shard_map/pallas_call | solution.py:417
  347.8 18.5 %shard_map.328 = (bf16[3,512,1408]{2,1,0:T(8,128)(2,1)}, bf16[512,1024]{1,0:T(8,128)(2,1)}, f32[512,1024]{1,0:T(8,128)}) custom-call(bf16[4,528,128]{2,1,0:T(8,128)(2,1)} %bitcast.4.refs_0_, bf16[4,528,128]{2,1,0:T(8,128)(2,1)} %collective-permute-done.34.refs_1_, bf16[4,528,128]{2,1,0:T(8,128)(2,1)} %collective-permute-done.38.refs_2_, ...), custom_call_target="tpu_custom_call" | custom-call | flops 8858370048 | bytes 14942208 | tf_op jit(solution)/shard_map/pallas_call | solution.py:417
  374.8 8.0 %shard_map.344 = (bf16[2,4,528,128]{3,2,1,0:T(8,128)(2,1)}, bf16[2,4,528,128]{3,2,1,0:T(8,128)(2,1)}, bf16[2,4,528,128]{3,2,1,0:T(8,128)(2,1)}, bf16[2,4,528,128]{3,2,1,0:T(8,128)(2,1)}) custom-call(bf16[3,512,1408]{2,1,0:T(8,128)(2,1)} %get-tuple-element.289.refs_0_, bf16[512,1024]{1,0:T(8,128)(2,1)} %get-tuple-element.213.refs_16_.refs_1_, ...), custom_call_target="tpu_custom_call" | custom-call | flops 2214592512 | bytes 12976128 | tf_op jit(solution)/shard_map/pallas_call | solution.py:588
  386.6 7.2 %shard_map.331 = (f32[512,1024]{1,0:T(8,128)}, bf16[512,1024]{1,0:T(8,128)(2,1)}, bf16[512,1024]{1,0:T(8,128)(2,1)}, f32[1,1024]{1,0:T(1,128)}) custom-call(bf16[4,512,128]{2,1,0:T(8,128)(2,1)} %bitcast.190, bf16[4,512,128]{2,1,0:T(8,128)(2,1)} %copy-done.13, bf16[4,512,128]{2,1,0:T(8,128)(2,1)} %copy-done.11, ...), custom_call_target="tpu_custom_call" | custom-call | flops 1073741824 | bytes 9441280 | tf_op jit(solution)/shard_map/pallas_call | solution.py:417
  393.8 13.8 %cross_bwd.1 = (bf16[512,1024]{1,0:T(8,128)(2,1)}, bf16[384,2048]{1,0:T(8,128)(2,1)}) custom-call(bf16[512,1024]{1,0:T(8,128)(2,1)} %get-tuple-element.205.q, bf16[384,2048]{1,0:T(8,128)(2,1)} %shard_map.325.k.v, bf16[384,2048]{1,0:T(8,128)(2,1)} %shard_map.325.k.v, bf16[512,1024]{1,0:T(8,128)(2,1)} %get-tuple-element.244.grad, ...), custom_call_target="tpu_custom_call" | custom-call | flops 4026531840 | bytes 6291456 | tf_op jit(solution)/shard_map/cross_bwd/pallas_call | solution.py:332
  418.1 9.0 %shard_map.332 = (f32[512,1024]{1,0:T(8,128)}, bf16[512,1024]{1,0:T(8,128)(2,1)}, bf16[512,1024]{1,0:T(8,128)(2,1)}, f32[1,1024]{1,0:T(1,128)}) custom-call(bf16[4,512,128]{2,1,0:T(8,128)(2,1)} %bitcast.191, bf16[4,512,128]{2,1,0:T(8,128)(2,1)} %copy-done.13, bf16[4,512,128]{2,1,0:T(8,128)(2,1)} %copy-done.11, ...), custom_call_target="tpu_custom_call" | custom-call | flops 2147483648 | bytes 13635584 | tf_op jit(solution)/shard_map/pallas_call | solution.py:417
  428.1 8.0 %shard_map.330 = (bf16[2,4,528,128]{3,2,1,0:T(8,128)(2,1)}, bf16[2,4,528,128]{3,2,1,0:T(8,128)(2,1)}, bf16[2,4,528,128]{3,2,1,0:T(8,128)(2,1)}, bf16[2,4,528,128]{3,2,1,0:T(8,128)(2,1)}) custom-call(bf16[3,512,1408]{2,1,0:T(8,128)(2,1)} %get-tuple-element.229.refs_0_, bf16[512,1024]{1,0:T(8,128)(2,1)} %get-tuple-element.213.refs_16_.refs_1_, ...), custom_call_target="tpu_custom_call" | custom-call | flops 2214592512 | bytes 12976128 | tf_op jit(solution)/shard_map/pallas_call | solution.py:588
  442.3 23.6 %self_bwd.1 = (bf16[512,1024]{1,0:T(8,128)(2,1)}, bf16[512,2048]{1,0:T(8,128)(2,1)}, bf16[512,2048]{1,0:T(8,128)(2,1)}, f32[8,64,512]{2,1,0:T(8,128)}) custom-call(s32[1]{0:T(128)} %bitcast.29.core, bf16[512,1024]{1,0:T(8,128)(2,1)} %shard_map.323.q, bf16[512,2048]{1,0:T(8,128)(2,1)} %get-tuple-element.201.k_own.v_own, ...), custom_call_target="tpu_custom_call" | custom-call | flops 8053063680 | bytes 20971520 | tf_op jit(solution)/shard_map/self_bwd/pallas_call | solution.py:244
  495.9 12.1 %collective-permute-done.101.refs_5_ = bf16[4,528,128]{2,1,0:T(8,128)(2,1)S(1)} collective-permute-done((bf16[4,528,128]{2,1,0:T(8,128)(2,1)S(1)}, bf16[4,528,128]{2,1,0:T(8,128)(2,1)S(1)}, u32[]{:S(2)}, u32[]{:S(2)}) %collective-permute-start.101) | collective-permute-done | bytes 540704 | tf_op jit(solution)/shard_map/ppermute | solution.py:1274
  554.0 10.4 %shard_map.333 = (bf16[512,1024]{1,0:T(8,128)(2,1)}, f32[1,1024]{1,0:T(1,128)}) custom-call(bf16[4,512,128]{2,1,0:T(8,128)(2,1)} %bitcast.184, bf16[4,512,128]{2,1,0:T(8,128)(2,1)} %copy-done.6, bf16[4,512,128]{2,1,0:T(8,128)(2,1)} %copy-done.4, bf16[4,512,128]{2,1,0:T(8,128)(2,1)} %copy-done.7, bf16[4,512,128]{2,1,0:T(8,128)(2,1)} %copy-done.5, ...), custom_call_target="tpu_custom_call" | custom-call | flops 3221225472 | bytes 14684160 | tf_op jit(solution)/shard_map/pallas_call | solution.py:417
  576.8 13.5 %collective-permute-done.98.refs_2_ = bf16[4,512,128]{2,1,0:T(8,128)(2,1)S(1)} collective-permute-done((bf16[4,512,128]{2,1,0:T(8,128)(2,1)}, bf16[4,512,128]{2,1,0:T(8,128)(2,1)S(1)}, u32[]{:S(2)}, u32[]{:S(2)}) %collective-permute-start.98) | collective-permute-done | bytes 524320 | tf_op jit(solution)/shard_map/ppermute | solution.py:1274
  610.0 27.2 %collective-permute-done.81 = bf16[128,1024]{1,0:T(8,128)(2,1)S(1)} collective-permute-done((bf16[128,1024]{1,0:T(8,128)(2,1)}, bf16[128,1024]{1,0:T(8,128)(2,1)S(1)}, u32[]{:S(2)}, u32[]{:S(2)}) %collective-permute-start.81) | collective-permute-done | bytes 262176 | tf_op jit(solution)/shard_map/ppermute | solution.py:1274
  652.8 11.8 %collective-permute-done.76 = bf16[128,1024]{1,0:T(8,128)(2,1)} collective-permute-done((bf16[128,1024]{1,0:T(8,128)(2,1)}, bf16[128,1024]{1,0:T(8,128)(2,1)}, u32[]{:S(2)}, u32[]{:S(2)}) %collective-permute-start.76) | collective-permute-done | bytes 262176 | tf_op jit(solution)/shard_map/ppermute | solution.py:1274
  (559 shorter events, 375.6 us)
Async XLA Ops:
  12.0 68.6 %all-gather.9.cloned.1.call-start = ((), (), s32[]{:S(2)}) async-start(), calls=%async_computation.8 | async-start | bytes 1351680 | tf_op jit(solution)/shard_map/all_gather | solution.py:1371
  16.5 101.5 %all-gather.13.cloned.1.call-start = ((), (), s32[]{:S(2)}) async-start(), calls=%async_computation.10 | async-start | bytes 1310720 | tf_op jit(solution)/shard_map/all_gather | solution.py:1371
  19.4 140.0 %all-gather.15.cloned.1.call-start = ((), (), s32[]{:S(2)}) async-start(), calls=%async_computation.11 | async-start | bytes 1351680 | tf_op jit(solution)/shard_map/all_gather | solution.py:1371
  21.1 491.0 %reduce-scatter.5.cloned.1.call-start = ((), (), s32[]{:S(2)}) async-start(), calls=%async_computation.4 | async-start | bytes 1351680 | tf_op jit(solution)/shard_map/reduce_scatter | solution.py:1383
  224.3 45.5 %collective-permute-start.58 = (bf16[512,2048]{1,0:T(8,128)(2,1)}, bf16[512,2048]{1,0:T(8,128)(2,1)}, u32[]{:S(2)}, u32[]{:S(2)}) collective-permute-start(bf16[512,2048]{1,0:T(8,128)(2,1)} %get-tuple-element.201.k_own.v_own), channel_id=1, source_target_pairs={{0,8},{1,9},{2,10},{3,11},{4,12},{5,13},{6,14},{7,15},{8,0},{9,1},... | collective-permute-start | bytes 6291464 | tf_op jit(solution)/shard_map/ppermute | solution.py:1274
  268.7 41.9 %collective-permute-start.66 = (bf16[4,528,128]{2,1,0:T(8,128)(2,1)}, bf16[4,528,128]{2,1,0:T(8,128)(2,1)S(1)}, u32[]{:S(2)}, u32[]{:S(2)}) collective-permute-start(bf16[4,528,128]{2,1,0:T(8,128)(2,1)} %collective-permute-done.14.refs_2_), channel_id=1, source_target_pairs={{0,8},{1,9},{2,10},{3,11},{4,12},{5,13},{6,14},{7,15},{8,0},{9,1},... | collective-permute-start | bytes 1622024 | tf_op jit(solution)/shard_map/ppermute | solution.py:1274
  269.3 41.4 %collective-permute-start.67 = (bf16[4,528,128]{2,1,0:T(8,128)(2,1)}, bf16[4,528,128]{2,1,0:T(8,128)(2,1)S(1)}, u32[]{:S(2)}, u32[]{:S(2)}) collective-permute-start(bf16[4,528,128]{2,1,0:T(8,128)(2,1)} %collective-permute-done.29.refs_3_), channel_id=1, source_target_pairs={{0,8},{1,9},{2,10},{3,11},{4,12},{5,13},{6,14},{7,15},{8,0},{9,1},... | collective-permute-start | bytes 1622024 | tf_op jit(solution)/shard_map/ppermute | solution.py:1274
  269.4 41.3 %collective-permute-start.68 = (bf16[4,528,128]{2,1,0:T(8,128)(2,1)}, bf16[4,528,128]{2,1,0:T(8,128)(2,1)}, u32[]{:S(2)}, u32[]{:S(2)}) collective-permute-start(bf16[4,528,128]{2,1,0:T(8,128)(2,1)} %collective-permute-done.30.refs_9_), channel_id=1, source_target_pairs={{0,8},{1,9},{2,10},{3,11},{4,12},{5,13},{6,14},{7,15},{8,0},{9,1},... | collective-permute-start | bytes 1622024 | tf_op jit(solution)/shard_map/ppermute | solution.py:1274
  269.8 40.9 %collective-permute-start.69 = (bf16[4,528,128]{2,1,0:T(8,128)(2,1)}, bf16[4,528,128]{2,1,0:T(8,128)(2,1)}, u32[]{:S(2)}, u32[]{:S(2)}) collective-permute-start(bf16[4,528,128]{2,1,0:T(8,128)(2,1)} %collective-permute-done.31.refs_11_), channel_id=1, source_target_pairs={{0,8},{1,9},{2,10},{3,11},{4,12},{5,13},{6,14},{7,15},{8,0},{9,1},... | collective-permute-start | bytes 1622024 | tf_op jit(solution)/shard_map/ppermute | solution.py:1274
  287.2 50.8 %collective-permute-start.44 = (bf16[4,528,128]{2,1,0:T(8,128)(2,1)}, bf16[4,528,128]{2,1,0:T(8,128)(2,1)}, u32[]{:S(2)}, u32[]{:S(2)}) collective-permute-start(bf16[4,528,128]{2,1,0:T(8,128)(2,1)} %collective-permute-done.38.refs_2_), channel_id=1, source_target_pairs={{0,8},{1,9},{2,10},{3,11},{4,12},{5,13},{6,14},{7,15},{8,0},{9,1},... | collective-permute-start | bytes 1622024 | tf_op jit(solution)/shard_map/ppermute | solution.py:1274
  372.9 55.2 %collective-permute-start.70 = (bf16[4,4,528,128]{3,2,1,0:T(8,128)(2,1)}, bf16[4,4,528,128]{3,2,1,0:T(8,128)(2,1)}, u32[]{:S(2)}, u32[]{:S(2)}) collective-permute-start(bf16[4,4,528,128]{3,2,1,0:T(8,128)(2,1)} %get-tuple-element.230), channel_id=1, source_target_pairs={{0,8},{1,9},{2,10},{3,11},{4,12},{5,13},{6,14},{7,15},{8,0},{9,1},... | collective-permute-start | bytes 6488072 | tf_op jit(solution)/shard_map/ppermute | solution.py:1274
  373.3 54.8 %collective-permute-start.71 = (bf16[4,4,528,128]{3,2,1,0:T(8,128)(2,1)}, bf16[4,4,528,128]{3,2,1,0:T(8,128)(2,1)}, u32[]{:S(2)}, u32[]{:S(2)}) collective-permute-start(bf16[4,4,528,128]{3,2,1,0:T(8,128)(2,1)} %get-tuple-element.231), channel_id=1, source_target_pairs={{0,8},{1,9},{2,10},{3,11},{4,12},{5,13},{6,14},{7,15},{8,0},{9,1},... | collective-permute-start | bytes 6488072 | tf_op jit(solution)/shard_map/ppermute | solution.py:1274
  412.0 107.1 %collective-permute-start.96 = (bf16[4,4,512,128]{3,2,1,0:T(8,128)(2,1)}, bf16[4,4,512,128]{3,2,1,0:T(8,128)(2,1)}, u32[]{:S(2)}, u32[]{:S(2)}) collective-permute-start(bf16[4,4,512,128]{3,2,1,0:T(8,128)(2,1)} %shard_map.341), channel_id=1, source_target_pairs={{0,8},{1,9},{2,10},{3,11},{4,12},{5,13},{6,14},{7,15},{8,0},{9,1},... | collective-permute-start | bytes 6291464 | tf_op jit(solution)/shard_map/ppermute | solution.py:1274
  442.2 153.8 %reduce-scatter.7.cloned.1.call-start = ((), (), s32[]{:S(2)}) async-start(), calls=%async_computation.5 | async-start | bytes 1351680 | tf_op jit(solution)/shard_map/reduce_scatter | solution.py:1383
  465.9 48.9 %collective-permute-start.78 = (bf16[512,2048]{1,0:T(8,128)(2,1)}, bf16[512,2048]{1,0:T(8,128)(2,1)}, u32[]{:S(2)}, u32[]{:S(2)}) collective-permute-start(bf16[512,2048]{1,0:T(8,128)(2,1)} %get-tuple-element.252), channel_id=1, source_target_pairs={{0,8},{1,9},{2,10},{3,11},{4,12},{5,13},{6,14},{7,15},{8,0},{9,1},... | collective-permute-start | bytes 6291464 | tf_op jit(solution)/shard_map/ppermute | solution.py:1274
  471.6 55.3 %collective-permute-start.94 = (bf16[4,4,512,128]{3,2,1,0:T(8,128)(2,1)}, bf16[4,4,512,128]{3,2,1,0:T(8,128)(2,1)}, u32[]{:S(2)}, u32[]{:S(2)}) collective-permute-start(bf16[4,4,512,128]{3,2,1,0:T(8,128)(2,1)} %shard_map.339), channel_id=1, source_target_pairs={{0,8},{1,9},{2,10},{3,11},{4,12},{5,13},{6,14},{7,15},{8,0},{9,1},... | collective-permute-start | bytes 6291464 | tf_op jit(solution)/shard_map/ppermute | solution.py:1274
  485.5 62.5 %collective-permute-start.90 = (bf16[4,4,512,128]{3,2,1,0:T(8,128)(2,1)}, bf16[4,4,512,128]{3,2,1,0:T(8,128)(2,1)}, u32[]{:S(2)}, u32[]{:S(2)}) collective-permute-start(bf16[4,4,512,128]{3,2,1,0:T(8,128)(2,1)} %shard_map.337), channel_id=1, source_target_pairs={{0,8},{1,9},{2,10},{3,11},{4,12},{5,13},{6,14},{7,15},{8,0},{9,1},... | collective-permute-start | bytes 6291464 | tf_op jit(solution)/shard_map/ppermute | solution.py:1274
  513.2 157.5 %reduce-scatter.9.cloned.1.call-start = ((), (), s32[]{:S(2)}) async-start(), calls=%async_computation.6 | async-start | bytes 1310720 | tf_op jit(solution)/shard_map/reduce_scatter | solution.py:1383
  527.0 44.2 %collective-permute-start.97 = (bf16[2,4,512,128]{3,2,1,0:T(8,128)(2,1)}, bf16[2,4,512,128]{3,2,1,0:T(8,128)(2,1)S(1)}, u32[]{:S(2)}, u32[]{:S(2)}) collective-permute-start(bf16[2,4,512,128]{3,2,1,0:T(8,128)(2,1)} %get-tuple-element.277), channel_id=1, source_target_pairs={{0,16},{1,17},{2,18},{3,19},{4,20},{5,21},{6,22},{7,23},{8,24},{9,... | collective-permute-start | bytes 3145736 | tf_op jit(solution)/shard_map/ppermute | solution.py:1274
  541.1 56.7 %collective-permute-start.88 = (bf16[4,4,512,128]{3,2,1,0:T(8,128)(2,1)}, bf16[4,4,512,128]{3,2,1,0:T(8,128)(2,1)}, u32[]{:S(2)}, u32[]{:S(2)}) collective-permute-start(bf16[4,4,512,128]{3,2,1,0:T(8,128)(2,1)} %shard_map.335), channel_id=1, source_target_pairs={{0,8},{1,9},{2,10},{3,11},{4,12},{5,13},{6,14},{7,15},{8,0},{9,1},... | collective-permute-start | bytes 6291464 | tf_op jit(solution)/shard_map/ppermute | solution.py:1274
  552.8 88.5 %collective-permute-start.91 = (bf16[2,4,512,128]{3,2,1,0:T(8,128)(2,1)}, bf16[2,4,512,128]{3,2,1,0:T(8,128)(2,1)S(1)}, u32[]{:S(2)}, u32[]{:S(2)}) collective-permute-start(bf16[2,4,512,128]{3,2,1,0:T(8,128)(2,1)} %get-tuple-element.263), channel_id=1, source_target_pairs={{0,16},{1,17},{2,18},{3,19},{4,20},{5,21},{6,22},{7,23},{8,24},{9,... | collective-permute-start | bytes 3145736 | tf_op jit(solution)/shard_map/ppermute | solution.py:1274
  597.7 100.5 %reduce-scatter.11.cloned.1.call-start = ((), (), s32[]{:S(2)}) async-start(), calls=%async_computation.7 | async-start | bytes 1310720 | tf_op jit(solution)/shard_map/reduce_scatter | solution.py:1383
  603.0 40.2 %collective-permute-start.89 = (bf16[2,4,512,128]{3,2,1,0:T(8,128)(2,1)}, bf16[2,4,512,128]{3,2,1,0:T(8,128)(2,1)S(1)}, u32[]{:S(2)}, u32[]{:S(2)}) collective-permute-start(bf16[2,4,512,128]{3,2,1,0:T(8,128)(2,1)} %get-tuple-element.261), channel_id=1, source_target_pairs={{0,4},{1,5},{2,6},{3,7},{4,0},{5,1},{6,2},{7,3},{8,12},{9,13},{10,... | collective-permute-start | bytes 3145736 | tf_op jit(solution)/shard_map/ppermute | solution.py:1274
  605.7 42.5 %collective-permute-start.74 = (bf16[128,1024]{1,0:T(8,128)(2,1)}, bf16[128,1024]{1,0:T(8,128)(2,1)}, u32[]{:S(2)}, u32[]{:S(2)}) collective-permute-start(bf16[128,1024]{1,0:T(8,128)(2,1)} %get-tuple-element.239), channel_id=1, source_target_pairs={{0,0},{1,1},{2,6},{3,7},{4,8},{5,9},{6,14},{7,15},{8,4},{9,5},{10,... | collective-permute-start | bytes 786440 | tf_op jit(solution)/shard_map/ppermute | solution.py:1274
  (170 other events, 2973.3 us)
Sparse Core Ops, SparseCore 0:
  12.1 30.6 all-gather.10
  45.0 28.0 all-gather.8
  75.2 42.7 all-gather.12
  120.0 39.2 all-gather.14
  442.4 27.8 reduce-scatter.4
  513.3 31.2 reduce-scatter.6
  597.9 39.2 reduce-scatter.8
  672.5 25.7 reduce-scatter.10
